TPU v7x, 256 devices: a whole 4x4x8 slice. The times are simulated.
256 devices in a mesh: space: 64 (over z, y, core), view: 4 (over x).
Axes of the slice: x: 4, y: 4, z: 8, core: 2. Of those that a mesh axis runs over, the one named last changes fastest.
Arguments:
- params: float32 [59, 131072], P(None, 'space'), may hold values from -8 to 1026, as said below
- visible: int32 [64, 128, 16], P('space'), may hold values from 0 to 2047, as said below
- blocks: int32 [64, 128], P('space'), may hold values from 0 to 63, as said below
- counts: int32 [64, 64], P('space'), may hold values from 1 to 2
- depth_rank: int32 [4, 64], P('view'), may hold values from 0 to 63, each once within a row
- camera: float32 [4, 3], P('view'), may hold values from -0.006 to 0.006
- background: float32 [4, 3], P('view'), may hold values from 0 to 1
- target: float32 [4, 3, 1024, 512], P('view', None, 'space'), may hold values from 0 to 1
Outputs:
- grad_params: float32 [59, 131072], P(None, 'space')
- rendered: float32 [4, 3, 1024, 512], P('view', None, 'space')
- loss: float32 [4], P('view')
Inputs may be any that keep to these rules, and one draw needn't show every extreme that they name: `visible`: each row of a subspace's table lists 16 different splats of that subspace in increasing order; every splat of the subspace is listed exactly once. Slot j of a subspace goes to owner j // 2; the 2 slots that one subspace sends to one owner name different blocks. counts[s, o] live slots lead the 2 slots that subspace s sends to owner o. `params`: rows 6 to 9 of a column hold a quaternion whose first component lies in [1, 2].
All inputs are finite; a program needn't handle non-finite values.
Results may differ from a plain program's by a relative error of at most 0.0003.
Values sent between devices are 32-bit elements; how exact they have to be, the bound alone decides.
No kernel may reach another device: no remote copies, remote signals or barrier semaphores. Data moves between devices by JAX's collectives and lax.ppermute only.
A program may use at most 64 MiB of HBM per device.

v0:
```python
import math

import jax
import jax.numpy as jnp
from jax import lax
from jax.experimental import pallas as pl
from jax.experimental.pallas import tpu as pltpu
from jax.sharding import PartitionSpec as P

F32 = jnp.float32
BF16 = jnp.bfloat16
I32 = jnp.int32

SH_ZERO = 0.28209479177387814
SH_ONE = 0.4886025119029199
SH_TWO = (
    1.0925484305920792,
    -1.0925484305920792,
    0.31539156525252005,
    -1.0925484305920792,
    0.5462742152960396,
)
SH_THREE = (
    -0.5900435899266435,
    2.890611442640554,
    -0.4570457994644658,
    0.3731763325901154,
    -0.4570457994644658,
    1.445305721320277,
    -0.5900435899266435,
)
DILATION = 0.3
SMOOTHING = 0.0001
SSIM_FIRST = 0.0001
SSIM_SECOND = 0.0009

K = 16
LANES = 128
CHUNKS = 4
GROUP = 4
META = 144
TABLE = 152


def taps():
    raw = [math.exp(-(offset - 5) * (offset - 5) / 4.5) for offset in range(11)]
    total = sum(raw)
    return [value / total for value in raw]


TAPS = taps()


def iota(shape, axis):
    return lax.broadcasted_iota(I32, shape, axis)


def row(x, index, rows):
    return jnp.broadcast_to(x[index : index + 1, :], (rows, x.shape[1]))


def turn_of(angles):
    cos_a, cos_b, cos_c = (jnp.cos(angle) for angle in angles)
    sin_a, sin_b, sin_c = (jnp.sin(angle) for angle in angles)
    return [
        [cos_c * cos_b, cos_c * sin_b * sin_a - sin_c * cos_a, cos_c * sin_b * cos_a + sin_c * sin_a],
        [sin_c * cos_b, sin_c * sin_b * sin_a + cos_c * cos_a, sin_c * sin_b * cos_a - cos_c * sin_a],
        [-sin_b, cos_b * sin_a, cos_b * cos_a],
    ]


def harmonics(axis):
    x, y, z = axis
    xx, yy, zz = (x * x, y * y, z * z)
    return [
        SH_ZERO * jnp.ones_like(x),
        -SH_ONE * y,
        SH_ONE * z,
        -SH_ONE * x,
        SH_TWO[0] * x * y,
        SH_TWO[1] * y * z,
        SH_TWO[2] * (2.0 * zz - xx - yy),
        SH_TWO[3] * x * z,
        SH_TWO[4] * (xx - yy),
        SH_THREE[0] * y * (3.0 * xx - yy),
        SH_THREE[1] * x * y * z,
        SH_THREE[2] * y * (4.0 * zz - xx - yy),
        SH_THREE[3] * z * (2.0 * zz - 3.0 * xx - 3.0 * yy),
        SH_THREE[4] * x * (4.0 * zz - xx - yy),
        SH_THREE[5] * z * (xx - yy),
        SH_THREE[6] * x * (xx - 3.0 * yy),
    ]


def camera_values(rows):
    angles = [jnp.broadcast_to(rows[i : i + 1, :], (8, LANES)) for i in range(3)]
    turn = turn_of(angles)
    basis = harmonics(turn[2])
    cell = lambda value: value[0:1, 0:1]
    return [[cell(value) for value in line] for line in turn], [cell(value) for value in basis]


def load_params(p_ref, scratch):
    for tile in range(8):
        count = min(8, 59 - tile * 8)
        for chunk in range(16):
            scratch[tile, chunk * 8 : chunk * 8 + count, :] = p_ref[
                tile * 8 : tile * 8 + count, chunk * LANES : (chunk + 1) * LANES
            ]


def dense_row(scratch, index):
    return scratch[index // 8, pl.ds(index % 8, 16, stride=8), :]


def spin_of(quaternion):
    w, x, y, z = quaternion
    return [
        [1.0 - 2.0 * (y * y + z * z), 2.0 * (x * y - w * z), 2.0 * (x * z + w * y)],
        [2.0 * (x * y + w * z), 1.0 - 2.0 * (x * x + z * z), 2.0 * (y * z - w * x)],
        [2.0 * (x * z - w * y), 2.0 * (y * z + w * x), 1.0 - 2.0 * (x * x + y * y)],
    ]


def sigmoid(x):
    return 1.0 / (1.0 + jnp.exp(-x))


def unit(quaternion):
    total = sum(part * part for part in quaternion)
    inverse = 1.0 / jnp.sqrt(total)
    return [part * inverse for part in quaternion], inverse


def slot_lists(vis_ref):
    natural = vis_ref[0].T
    lane = iota((K, LANES), 1)
    order = (lane % 64) * 2 + lane // 64
    return jnp.take_along_axis(natural, order, axis=1), order


def to_message(out_ref, table):
    first = table[0:LANES, :].T
    rest = jnp.concatenate(
        [table[LANES:TABLE, :], jnp.zeros((2 * LANES - TABLE, LANES), F32)], axis=0
    ).T
    out_ref[:, 0:LANES] = first[0:64]
    out_ref[:, LANES : 2 * LANES] = first[64:128]
    out_ref[:, 2 * LANES : 3 * LANES] = rest[0:64] + pltpu.roll(rest[64:128], 64, 1)


def from_message(in_ref):
    first = jnp.concatenate([in_ref[:, 0:LANES], in_ref[:, LANES : 2 * LANES]], axis=0).T
    both = in_ref[:, 2 * LANES : 3 * LANES]
    rest = jnp.concatenate([both, pltpu.roll(both, 64, 1)], axis=0)
    return first, rest.T, rest


def send_kernel(p_ref, cam_ref, vis_ref, blk_ref, cnt_ref, rank_ref, out_ref, par, rec):
    me = lax.axis_index("space")
    load_params(p_ref, par)
    cam = jnp.broadcast_to(cam_ref[...], (8, 3))
    rows = jnp.concatenate(
        [jnp.broadcast_to(cam[0:1, i : i + 1], (1, LANES)) for i in range(3)]
        + [jnp.zeros((5, LANES), F32)],
        axis=0,
    )
    turn, basis = camera_values(rows)
    get = lambda index: dense_row(par, index)
    scales = [jnp.exp(get(3 + i)) for i in range(3)]
    quaternion, _ = unit([get(6 + i) for i in range(4)])
    spin = spin_of(quaternion)
    frame = [
        [
            (turn[r][0] * spin[0][c] + turn[r][1] * spin[1][c] + turn[r][2] * spin[2][c]) * scales[c]
            for c in range(3)
        ]
        for r in range(2)
    ]
    cov_xx = sum(frame[0][c] * frame[0][c] for c in range(3)) + DILATION
    cov_xy = sum(frame[0][c] * frame[1][c] for c in range(3))
    cov_yy = sum(frame[1][c] * frame[1][c] for c in range(3)) + DILATION
    inverse = 1.0 / (cov_xx * cov_yy - cov_xy * cov_xy)
    shift_x = get(0) - 256.0
    shift_y = get(1) - 512.0
    depth = get(2)
    rec[0:16, :] = turn[0][0] * shift_x + turn[0][1] * shift_y + turn[0][2] * depth + 256.0
    rec[16:32, :] = turn[1][0] * shift_x + turn[1][1] * shift_y + turn[1][2] * depth + 512.0
    rec[32:48, :] = cov_yy * inverse
    rec[48:64, :] = -cov_xy * inverse
    rec[64:80, :] = cov_xx * inverse
    rec[80:96, :] = sigmoid(get(10))
    for c in range(3):
        colour = jnp.full((16, LANES), 0.5, F32)
        for k in range(16):
            colour = colour + basis[k] * get(11 + 3 * k + c)
        rec[96 + 16 * c : 112 + 16 * c, :] = colour
    lists, order = slot_lists(vis_ref)
    low = lists & 127
    high = lists // LANES
    channels = []
    for ch in range(9):
        value = jnp.zeros((K, LANES), F32)
        for h in range(16):
            source = jnp.broadcast_to(rec[ch * 16 + h : ch * 16 + h + 1, :], (K, LANES))
            value = jnp.where(high == h, jnp.take_along_axis(source, low, axis=1), value)
        channels.append(value)
    blk = jnp.take_along_axis(jnp.broadcast_to(blk_ref[...], (8, LANES)), order[0:8], axis=1)
    counts = jnp.concatenate([cnt_ref[...], cnt_ref[...]], axis=1)
    ids = jnp.where(iota((8, LANES), 1) // 64 < counts, blk, -1).astype(F32)
    rank = jnp.sum(
        jnp.where(iota((1, 64), 1) == me, rank_ref[...], 0).astype(F32), axis=1, keepdims=True
    )
    meta = jnp.where(iota((8, LANES), 0) == 0, ids, jnp.broadcast_to(rank, (8, LANES)))
    to_message(out_ref, jnp.concatenate(channels + [meta], axis=0))


def shift_right(chunks, amount, lane):
    turned = [pltpu.roll(x, amount, 1) for x in chunks]
    return [
        jnp.where(lane < amount, turned[j - 1] if j else 0.0, turned[j]) for j in range(CHUNKS)
    ]


def shift_left(chunks, amount, lane):
    turned = [pltpu.roll(x, LANES - amount, 1) for x in chunks]
    return [
        jnp.where(lane >= LANES - amount, turned[j + 1] if j < CHUNKS - 1 else 0.0, turned[j])
        for j in range(CHUNKS)
    ]


def across(chunks):
    lane = iota(chunks[0].shape, 1)
    total = [TAPS[5] * x for x in chunks]
    for s in range(1, 6):
        right = shift_right(chunks, s, lane)
        left = shift_left(chunks, s, lane)
        total = [t + TAPS[5 + s] * (a + b) for t, a, b in zip(total, right, left)]
    return total


def down(load, start, count):
    total = TAPS[5] * load(start + 5, count)
    for s in range(1, 6):
        total = total + TAPS[5 + s] * (load(start + 5 - s, count) + load(start + 5 + s, count))
    return total


def fill_rows(ext, own, before, after, ch):
    for j in range(CHUNKS):
        cols = slice(j * LANES, (j + 1) * LANES)
        ext[j, 0:8, :] = jnp.zeros((8, LANES), F32)
        ext[j, 40:48, :] = jnp.zeros((8, LANES), F32)
        ext[j, 6:16, :] = before[ch, :, cols]
        ext[j, 16:32, :] = own[0, ch, :, cols]
        ext[j, 32:42, :] = after[ch, :, cols]


def target_kernel(own, before, after, vis_ref, ext_ref, mean_ref, square_ref, inv_ref, tmp, sq):
    def channel(ch, carry):
        fill_rows(tmp, own, before, after, ch)
        for j in range(CHUNKS):
            ext_ref[ch, j] = tmp[j]
            sq[j] = tmp[j] * tmp[j]
        for source, out in ((tmp, mean_ref), (sq, square_ref)):
            blurred = across(
                [down(lambda s, n: source[j, pl.ds(s, n), :], 6, 32) for j in range(CHUNKS)]
            )
            for j in range(CHUNKS):
                out[ch, j] = blurred[j]
        return carry

    lax.fori_loop(0, 3, channel, 0)
    lists, _ = slot_lists(vis_ref)
    low = lists & 127
    high = lists // LANES
    total = jnp.zeros((2 * 16, LANES), F32)
    lane = iota((1, LANES), 1)
    for k in range(K):
        here = row(high, k, 16) == iota((16, LANES), 0)
        value = jnp.concatenate(
            [
                jnp.where(here, float(k), 0.0),
                jnp.where(here, jnp.broadcast_to(lane, (16, LANES)).astype(F32), 0.0),
            ],
            axis=0,
        ).astype(BF16)
        table = (row(low, k, LANES) == iota((LANES, LANES), 0)).astype(F32).astype(BF16)
        total = total + lax.dot_general(
            value, table, (((1,), (1,)), ((), ())), preferred_element_type=F32
        )
    inv_ref[...] = total.astype(I32)


def pieces(x):
    first = x.astype(BF16)
    left = x - first.astype(F32)
    second = left.astype(BF16)
    third = (left - second.astype(F32)).astype(BF16)
    return first, second, third


def dot_mask(x, mask, contract):
    dims = (((1,), (contract,)), ((), ()))
    parts = [lax.dot_general(p, mask, dims, preferred_element_type=F32) for p in pieces(x)]
    return parts[0] + (parts[1] + parts[2])


def corners(ids, me):
    block = jnp.maximum(ids, 0.0).astype(I32)
    x = (block % 32 * 16).astype(F32) + 0.5
    y = (me * 16 + block // 32 * 8).astype(F32) + 0.5
    return x, y


def splat_terms(rec, k, x0, y_grid):
    get = lambda ch: jnp.broadcast_to(rec[pl.ds(ch * K + k, 1), :], (8, LANES))
    dy = y_grid - get(1)
    return x0 - get(0), dy, get(2) * -0.5, get(3) * dy, get(4) * -0.5 * dy * dy, get(5)


def blend_kernel(
    recv_ref,
    bg_ref,
    strip_ref,
    top_ref,
    bottom_ref,
    rec,
    colour_ref,
    before_ref,
    total_ref,
    nearer_ref,
    logs,
    blocks_ref,
):
    me = lax.axis_index("space")
    first, rest_rows, rest_cols = from_message(recv_ref)
    rec[0:LANES, :] = first
    rec[LANES:TABLE, :] = rest_rows[0:24]
    ids = row(rest_rows, 16, 8)
    corner_x, corner_y = corners(ids, me)
    y_grid = corner_y + iota((8, LANES), 0).astype(F32)

    def group(g, carry):
        base = corner_x + (g * GROUP).astype(F32)

        def four(kk, state):
            through, log_sum, colours = state
            part = [jnp.ones((8, LANES), F32)] * GROUP
            for k4 in range(4):
                k = kk * 4 + k4
                dx0, dy, ma, mb_y, mc_yy, opacity = splat_terms(rec, k, base, y_grid)
                tint = [jnp.broadcast_to(rec[pl.ds((6 + c) * K + k, 1), :], (8, LANES)) for c in range(3)]
                for i in range(GROUP):
                    dx = dx0 + float(i)
                    alpha = opacity * jnp.exp((ma * dx - mb_y) * dx + mc_yy)
                    weight = alpha * through[i]
                    keep = 1.0 - alpha
                    through = through[:i] + (through[i] * keep,) + through[i + 1 :]
                    part[i] = part[i] * keep
                    colours = (
                        colours[:i]
                        + (tuple(colours[i][c] + weight * tint[c] for c in range(3)),)
                        + colours[i + 1 :]
                    )
            log_sum = tuple(log_sum[i] + jnp.log(part[i]) for i in range(GROUP))
            return through, log_sum, colours

        zero = jnp.zeros((8, LANES), F32)
        _, log_sum, colours = lax.fori_loop(
            0,
            4,
            four,
            (
                (jnp.ones((8, LANES), F32),) * GROUP,
                (zero,) * GROUP,
                ((zero,) * 3,) * GROUP,
            ),
        )
        for i in range(GROUP):
            rows = pl.ds(pl.multiple_of((g * GROUP + i) * 8, 8), 8)
            logs[rows, :] = log_sum[i]
            for c in range(3):
                colour_ref[c, rows, :] = colours[i][c]
        return carry

    lax.fori_loop(0, 16 // GROUP, group, 0)
    id_row = row(rest_rows, 16, LANES)
    rank_row = row(rest_rows, 17, LANES)
    id_col = jnp.broadcast_to(rest_cols[:, 16:17], (LANES, LANES))
    rank_col = jnp.broadcast_to(rest_cols[:, 17:18], (LANES, LANES))
    live = id_row >= 0.0
    same = jnp.where((id_row == id_col) & live, 1.0, 0.0)
    nearer = jnp.where(rank_col < rank_row, same, 0.0).astype(BF16)
    member = jnp.where(id_col == iota((LANES, LANES), 1).astype(F32), 1.0, 0.0).astype(BF16)
    nearer_ref[...] = nearer
    log_all = logs[...]
    ahead = dot_mask(
        log_all, jnp.concatenate([nearer, same.astype(BF16), member], axis=1), 0
    )
    before = jnp.where(live, jnp.exp(ahead[:, 0:LANES]), 0.0)
    before_ref[...] = before
    total_ref[...] = jnp.where(live, jnp.exp(ahead[:, LANES : 2 * LANES]), 0.0)
    open_sky = jnp.exp(ahead[:, 2 * LANES : 3 * LANES])
    lane = iota((8, LANES), 1)
    for c in range(3):
        back = bg_ref[0:1, c : c + 1]
        blocks_ref[c] = dot_mask(before * colour_ref[c], member, 0) + back * open_sky
    for c in range(3):
        for br in range(2):
            for t in range(CHUNKS):
                index = br * 32 + 8 * t + lane // 16
                value = jnp.zeros((8, LANES), F32)
                for cc in range(16):
                    got = jnp.take_along_axis(blocks_ref[c, cc * 8 : cc * 8 + 8, :], index, axis=1)
                    value = jnp.where(lane % 16 == cc, got, value)
                strip_ref[0, c, br * 8 : br * 8 + 8, t * LANES : (t + 1) * LANES] = value
    top_ref[...] = strip_ref[0, :, 0:10, :]
    bottom_ref[...] = strip_ref[0, :, 6:16, :]


def loss_kernel(
    strip_ref,
    before_strip,
    after_strip,
    ext_ref,
    mean_ref,
    square_ref,
    bg_ref,
    rec,
    colour_ref,
    before_ref,
    total_ref,
    nearer_ref,
    out_ref,
    ext,
    prod,
    stat,
    grads,
    pulled,
    cot,
    log_cot,
    alphas,
    throughs,
    sums,
    table,
):
    me = lax.axis_index("space")
    t_row = iota((32, LANES), 0)
    where = me * 16 - 5 + t_row
    inside = jnp.where((where >= 0) & (where < 1024) & (t_row < 26), -0.2, 0.0)
    own = (t_row >= 5) & (t_row < 21)
    first_c, second_c = SSIM_FIRST, SSIM_SECOND

    def channel(ch, loss):
        fill_rows(ext, strip_ref, before_strip, after_strip, ch)
        for j in range(CHUNKS):
            a = ext[j]
            prod[0, j] = a * a
            prod[1, j] = a * ext_ref[ch, j]
        blurred = []
        for source in (ext, prod.at[0], prod.at[1]):
            blurred.append(
                across([down(lambda s, n: source[j, pl.ds(s, n), :], 6, 32) for j in range(CHUNKS)])
            )
        for j in range(CHUNKS):
            ma, mb = blurred[0][j], mean_ref[ch, j]
            mab = ma * mb
            squares = ma * ma + mb * mb
            n1 = 2.0 * mab + first_c
            n2 = 2.0 * (blurred[2][j] - mab) + second_c
            d1 = squares + first_c
            d2 = (blurred[1][j] + square_ref[ch, j]) - squares + second_c
            inverse = 1.0 / (d1 * d2)
            ssim = n1 * n2 * inverse
            loss = loss + jnp.where(own, 0.2 - 0.2 * ssim, 0.0)
            seed = inside * inverse
            g1 = seed * n2
            g2 = seed * n1
            scaled = inside * ssim
            gd1 = scaled * inverse * d2
            gd2 = scaled * inverse * d1
            stat[0, j] = 2.0 * (mb * (g1 - g2) + ma * (gd2 - gd1))
            stat[1, j] = -gd2
            stat[2, j] = 2.0 * g2
        spread = []
        for q in range(3):
            spread.append(
                across([down(lambda s, n: stat[q, j, pl.ds(s, n), :], 0, 16) for j in range(CHUNKS)])
            )
        for j in range(CHUNKS):
            a = ext[j, 16:32, :]
            b = ext_ref[ch, j, 16:32, :]
            differ = a - b
            root = jnp.sqrt(differ * differ + SMOOTHING)
            loss = loss + jnp.concatenate([0.8 * root, jnp.zeros((16, LANES), F32)], axis=0)
            grads[ch, j] = (
                spread[0][j] + 2.0 * a * spread[1][j] + b * spread[2][j] + 0.8 * differ / root
            )
        return loss

    loss = lax.fori_loop(0, 3, channel, jnp.zeros((32, LANES), F32))
    loss = jnp.sum(jnp.sum(loss, axis=0, keepdims=True), axis=1, keepdims=True)

    ids = row(rec[...], META, 8)
    live = ids >= 0.0
    block = jnp.maximum(ids, 0.0).astype(I32)
    place = block // 8
    start = block % 8 * 16
    for c in range(3):
        for cc in range(16):
            value = jnp.zeros((8, LANES), F32)
            for br in range(2):
                for t in range(CHUNKS):
                    got = jnp.take_along_axis(
                        grads[c, t, br * 8 : br * 8 + 8, :], start + cc, axis=1
                    )
                    value = jnp.where(place == br * 4 + t, got, value)
            pulled[c, cc * 8 : cc * 8 + 8, :] = jnp.where(live, value, 0.0)
    before = before_ref[...]
    behind = jnp.zeros((LANES, LANES), F32)
    sky = jnp.zeros((LANES, LANES), F32)
    for c in range(3):
        g = pulled[c]
        scaled = before * g
        cot[c] = scaled
        behind = behind + scaled * colour_ref[c]
        sky = sky + bg_ref[0:1, c : c + 1] * g
    log_cot[...] = dot_mask(behind, nearer_ref[...], 1) + total_ref[...] * sky

    corner_x, corner_y = corners(ids, me)
    y_grid = corner_y + iota((8, LANES), 0).astype(F32)

    def group(g, carry):
        base = corner_x + (g * GROUP).astype(F32)
        rows = [pl.ds(pl.multiple_of((g * GROUP + i) * 8, 8), 8) for i in range(GROUP)]
        through = [jnp.ones((8, LANES), F32)] * GROUP
        for k in range(K):
            dx0, dy, ma, mb_y, mc_yy, opacity = splat_terms(rec, k, base, y_grid)
            for i in range(GROUP):
                dx = dx0 + float(i)
                alpha = opacity * jnp.exp((ma * dx - mb_y) * dx + mc_yy)
                alphas[k, i] = alpha
                throughs[k, i] = through[i]
                through[i] = through[i] * (1.0 - alpha)

        suffix = tuple(log_cot[rows[i], :] for i in range(GROUP))
        pull = [[cot[c, rows[i], :] for c in range(3)] for i in range(GROUP)]
        zero = jnp.zeros((8, LANES), F32)

        def back(step, suffix):
            k = K - 1 - step
            get = lambda ch: jnp.broadcast_to(rec[pl.ds(ch * K + k, 1), :], (8, LANES))
            dx0 = base - get(0)
            tint = [get(6 + c) for c in range(3)]
            s0, s1, s2 = zero, zero, zero
            shade = [zero] * 3
            after = []
            for i in range(GROUP):
                dx = dx0 + float(i)
                alpha = alphas[k, i]
                seen = throughs[k, i]
                gain = seen * (
                    pull[i][0] * tint[0] + pull[i][1] * tint[1] + pull[i][2] * tint[2]
                )
                g_alpha = gain - suffix[i] / (1.0 - alpha)
                after.append(suffix[i] + alpha * gain)
                moment = alpha * g_alpha
                weight = alpha * seen
                shade = [shade[c] + weight * pull[i][c] for c in range(3)]
                moment_x = moment * dx
                s0 = s0 + moment
                s1 = s1 + moment_x
                s2 = s2 + moment_x * dx
            for n, value in enumerate([s0, s1, s2] + shade):
                sums[k, n] = jnp.where(g == 0, value, sums[k, n] + value)
            return tuple(after)

        lax.fori_loop(0, K, back, suffix)
        return carry

    lax.fori_loop(0, 16 // GROUP, group, 0)

    def finish(k, carry):
        get = lambda ch: rec[pl.ds(ch * K + k, 1), :]
        dy = y_grid - jnp.broadcast_to(get(1), (8, LANES))
        s0, s1, s2 = sums[k, 0], sums[k, 1], sums[k, 2]
        fold = lambda value: jnp.sum(value, axis=0, keepdims=True)
        s0_y = s0 * dy
        m0, mx, mxx = fold(s0), fold(s1), fold(s2)
        my, mxy, myy = fold(s0_y), fold(s1 * dy), fold(s0_y * dy)
        conic_a, conic_b, conic_c = get(2), get(3), get(4)
        out = [
            conic_a * mx + conic_b * my,
            conic_b * mx + conic_c * my,
            -0.5 * mxx,
            -mxy,
            -0.5 * myy,
            m0,
        ] + [fold(sums[k, 3 + c]) for c in range(3)]
        for ch in range(9):
            table[pl.ds(ch * K + k, 1), :] = out[ch]
        return carry

    lax.fori_loop(0, K, finish, 0)
    table[META:TABLE, :] = jnp.broadcast_to(loss, (8, LANES))
    to_message(out_ref, table[...])


def gather_kernel(recv_ref, inv_ref, cam_ref, out_ref, loss_ref, rec):
    first, rest_rows, rest_cols = from_message(recv_ref)
    rec[0:LANES, :] = first
    rec[LANES:META, :] = rest_rows[0:16]
    at_k = inv_ref[0:16, :]
    at_slot = inv_ref[16:32, :]
    for ch in range(9):
        value = jnp.zeros((16, LANES), F32)
        for k in range(K):
            source = jnp.broadcast_to(rec[ch * K + k : ch * K + k + 1, :], (16, LANES))
            value = jnp.where(at_k == k, jnp.take_along_axis(source, at_slot, axis=1), value)
        out_ref[ch * 16 : ch * 16 + 16, :] = value
    out_ref[META:TABLE, :] = jnp.concatenate(
        [jnp.broadcast_to(cam_ref[0:1, i : i + 1], (1, LANES)) for i in range(3)]
        + [jnp.zeros((5, LANES), F32)],
        axis=0,
    )
    total = jnp.sum(rest_cols[0:64, 16:17], axis=0, keepdims=True)
    loss_ref[...] = jnp.broadcast_to(total * (1.0 / 1572864.0), (1, LANES))


def pull_kernel(p_ref, rec0, rec1, rec2, rec3, out_ref, par, views, res):
    me = lax.axis_index("view")
    load_params(p_ref, par)
    for d, source in enumerate((rec0, rec1, rec2, rec3)):
        views[(me - d + 4) % 4] = source[...]
    get = lambda index: dense_row(par, index)
    scales = [jnp.exp(get(3 + i)) for i in range(3)]
    quaternion, inverse_norm = unit([get(6 + i) for i in range(4)])
    spin = spin_of(quaternion)
    zero = jnp.zeros((16, LANES), F32)
    g_pos = [zero] * 3
    g_frame_spin = [[zero] * 3 for _ in range(3)]
    g_log = [zero] * 3
    g_logit = zero
    g_colour = []
    bases = []
    for v in range(4):
        turn, basis = camera_values(views[v, META:TABLE, :])
        bases.append(basis)
        g = [views[v, ch * 16 : ch * 16 + 16, :] for ch in range(9)]
        unscaled = [
            [turn[r][0] * spin[0][c] + turn[r][1] * spin[1][c] + turn[r][2] * spin[2][c] for c in range(3)]
            for r in range(2)
        ]
        frame = [[unscaled[r][c] * scales[c] for c in range(3)] for r in range(2)]
        cov_xx = sum(frame[0][c] * frame[0][c] for c in range(3)) + DILATION
        cov_xy = sum(frame[0][c] * frame[1][c] for c in range(3))
        cov_yy = sum(frame[1][c] * frame[1][c] for c in range(3)) + DILATION
        inverse = 1.0 / (cov_xx * cov_yy - cov_xy * cov_xy)
        ca, cb, cc = cov_yy * inverse, -cov_xy * inverse, cov_xx * inverse
        ga, gb, gc = g[2], 0.5 * g[3], g[4]
        left = [
            [ca * ga + cb * gb, ca * gb + cb * gc],
            [cb * ga + cc * gb, cb * gb + cc * gc],
        ]
        g_xx = -(left[0][0] * ca + left[0][1] * cb)
        g_xy = -(left[0][0] * cb + left[0][1] * cc)
        g_yy = -(left[1][0] * cb + left[1][1] * cc)
        for c in range(3):
            gf0 = 2.0 * (g_xx * frame[0][c] + g_xy * frame[1][c])
            gf1 = 2.0 * (g_xy * frame[0][c] + g_yy * frame[1][c])
            g_log[c] = g_log[c] + gf0 * frame[0][c] + gf1 * frame[1][c]
            for m in range(3):
                g_frame_spin[m][c] = g_frame_spin[m][c] + (turn[0][m] * gf0 + turn[1][m] * gf1)
        for m in range(3):
            g_pos[m] = g_pos[m] + turn[0][m] * g[0] + turn[1][m] * g[1]
        g_logit = g_logit + g[5]
        g_colour.append(g[6:9])
    s = [[g_frame_spin[m][c] * scales[c] for c in range(3)] for m in range(3)]
    w, x, y, z = quaternion
    g_unit = [
        2.0 * (x * (s[2][1] - s[1][2]) + y * (s[0][2] - s[2][0]) + z * (s[1][0] - s[0][1])),
        2.0 * (y * (s[0][1] + s[1][0]) + z * (s[0][2] + s[2][0]) + w * (s[2][1] - s[1][2]))
        - 4.0 * x * (s[1][1] + s[2][2]),
        2.0 * (x * (s[0][1] + s[1][0]) + z * (s[1][2] + s[2][1]) + w * (s[0][2] - s[2][0]))
        - 4.0 * y * (s[0][0] + s[2][2]),
        2.0 * (x * (s[0][2] + s[2][0]) + y * (s[1][2] + s[2][1]) + w * (s[1][0] - s[0][1]))
        - 4.0 * z * (s[0][0] + s[1][1]),
    ]
    along = sum(q * g for q, g in zip(quaternion, g_unit))
    g_quat = [(g - q * along) * inverse_norm for q, g in zip(quaternion, g_unit)]
    rest = sigmoid(-get(10))
    rows = g_pos + g_log + g_quat + [g_logit * rest]
    for k in range(16):
        for c in range(3):
            total = bases[0][k] * g_colour[0][c]
            for v in range(1, 4):
                total = total + bases[v][k] * g_colour[v][c]
            rows.append(total)
    for index in range(59):
        res[index // 8, pl.ds(index % 8, 16, stride=8), :] = rows[index]
    for tile in range(8):
        count = min(8, 59 - tile * 8)
        for chunk in range(16):
            out_ref[tile * 8 : tile * 8 + count, chunk * LANES : (chunk + 1) * LANES] = res[
                tile, chunk * 8 : chunk * 8 + count, :
            ]


def call(kernel, outs, scratch=(), vmem=None):
    return pl.pallas_call(
        kernel,
        out_shape=[jax.ShapeDtypeStruct(shape, dtype) for shape, dtype in outs],
        scratch_shapes=[pltpu.VMEM(shape, dtype) for shape, dtype in scratch],
        compiler_params=pltpu.CompilerParams(vmem_limit_bytes=vmem or 16 << 20),
    )


def shards(params, visible, blocks, counts, depth_rank, camera, background, target):
    devices = lax.axis_size("space")
    views = lax.axis_size("view")
    up = [(i, i + 1) for i in range(devices - 1)]
    below = [(i + 1, i) for i in range(devices - 1)]
    tile = (LANES, LANES)

    goal_before = lax.ppermute(target[0, :, 6:16], "space", up)
    goal_after = lax.ppermute(target[0, :, 0:10], "space", below)
    (message,) = call(
        send_kernel,
        [((64, 384), F32)],
        [((8, LANES, LANES), F32), ((META, LANES), F32)],
    )(params, camera, visible, blocks, counts, depth_rank)
    received = lax.all_to_all(message, "space", 0, 0, tiled=True)
    goal, goal_mean, goal_square, inverse = call(
        target_kernel,
        [
            ((3, CHUNKS, 48, LANES), F32),
            ((3, CHUNKS, 32, LANES), F32),
            ((3, CHUNKS, 32, LANES), F32),
            ((32, LANES), I32),
        ],
        [((CHUNKS, 48, LANES), F32)] * 2,
    )(target, goal_before, goal_after, visible)
    strip, top, bottom, records, colours, before, total, nearer = call(
        blend_kernel,
        [
            ((1, 3, 16, 512), F32),
            ((3, 10, 512), F32),
            ((3, 10, 512), F32),
            ((TABLE, LANES), F32),
            ((3, *tile), F32),
            (tile, F32),
            (tile, F32),
            (tile, BF16),
        ],
        [(tile, F32), ((3, *tile), F32)],
    )(received, background)
    strip_before = lax.ppermute(bottom, "space", up)
    strip_after = lax.ppermute(top, "space", below)
    (reply,) = call(
        loss_kernel,
        [((64, 384), F32)],
        [
            ((CHUNKS, 48, LANES), F32),
            ((2, CHUNKS, 48, LANES), F32),
            ((3, CHUNKS, 32, LANES), F32),
            ((3, CHUNKS, 16, LANES), F32),
            ((3, *tile), F32),
            ((3, *tile), F32),
            (tile, F32),
            ((K, GROUP, 8, LANES), F32),
            ((K, GROUP, 8, LANES), F32),
            ((K, 6, 8, LANES), F32),
            ((TABLE, LANES), F32),
        ],
    )(
        strip,
        strip_before,
        strip_after,
        goal,
        goal_mean,
        goal_square,
        background,
        records,
        colours,
        before,
        total,
        nearer,
    )
    returned = lax.all_to_all(reply, "space", 0, 0, tiled=True)
    record_grads, loss = call(
        gather_kernel,
        [((TABLE, LANES), F32), ((1, LANES), F32)],
        [((META, LANES), F32)],
    )(returned, inverse, camera)
    others = [
        lax.ppermute(record_grads, "view", [(i, (i + d) % views) for i in range(views)])
        for d in range(1, views)
    ]
    (grad_params,) = call(
        pull_kernel,
        [((59, 2048), F32)],
        [((8, LANES, LANES), F32), ((4, TABLE, LANES), F32), ((8, LANES, LANES), F32)],
    )(params, record_grads, *others)
    return (grad_params, strip, loss[0, 0:1])


def solution(mesh):
    in_specs = (
        P(None, "space"),
        P("space", None, None),
        P("space", None),
        P("space", None),
        P("view", None),
        P("view", None),
        P("view", None),
        P("view", None, "space", None),
    )
    out_specs = (P(None, "space"), P("view", None, "space", None), P("view"))
    return jax.shard_map(shards, mesh=mesh, in_specs=in_specs, out_specs=out_specs, check_vma=False)
```

profile of v0, /device:TPU:1, one launch (start us, length us, event | category | flops | bytes accessed | tf_op | source)
XLA Modules:
  0.0 78.2 jit_solution(6196595626340258997)
XLA Ops:
  0.7 0.8 %copy.13.vis_ref = s32[1,128,16]{2,1,0:T(8,128)S(1)} copy(s32[1,128,16]{1,2,0:T(8,128)} %param.9) | data formatting | bytes 16384 | tf_op args[1]
  1.5 0.0 copy-start
  1.5 1.0 %copy-done = f32[59,2048]{1,0:T(8,128)S(1)} copy-done((f32[59,2048]{1,0:T(8,128)S(1)}, f32[59,2048]{1,0:T(8,128)}, u32[]{:S(2)}) %copy-start) | copy-done | bytes 483352
  2.6 1.0 %shard_map.103 = f32[64,384]{1,0:T(8,128)S(1)} custom-call(f32[59,2048]{1,0:T(8,128)S(1)} %copy-done, f32[1,3]{1,0:T(1,128)S(1)} %copy-done.5, s32[1,128,16]{2,1,0:T(8,128)S(1)} %copy.13.vis_ref, s32[1,128]{1,0:T(1,128)S(1)} %copy-done.6, s32[1,64]{1,0:T(1,128)S(1)} %copy-done.7, s32[1,64]{1,0:T(1,128)S(1)} %copy-done.8), custom_call_target="tpu_custom_call" | custom-call | tf_op jit(solution)/shard_map/pallas_call | solution.py:729
  3.6 0.7 copy.14
  4.3 13.3 %all-to-all-start = ((f32[64,1,384]{2,1,0:T(1,128)}), f32[64,1,384]{2,1,0:T(1,128)S(1)}, u32[]{:S(2)}, u32[]{:S(2)}) async-start(f32[64,1,384]{2,1,0:T(1,128)} %copy.14), calls=%async_computation | async-start | bytes 196608 | tf_op jit(solution)/shard_map/all_to_all | solution.py:734
  17.6 2.4 %collective-permute-start.3 = (f32[3,10,512]{2,1,0:T(8,128)S(1)}, f32[3,10,512]{2,1,0:T(8,128)S(1)}, u32[]{:S(2)}, u32[]{:S(2)}) collective-permute-start(f32[3,10,512]{2,1,0:T(8,128)S(1)} %get-tuple-element.31), channel_id=1, source_target_pairs={{4,0},{8,4},{12,8},{16,12},{20,16},{24,20},{28,24},{32,28},{36,32}... | collective-permute-start | bytes 184328 | tf_op jit(solution)/shard_map/ppermute | solution.py:728
  20.0 3.2 %collective-permute-start.2 = (f32[3,10,512]{2,1,0:T(8,128)S(1)}, f32[3,10,512]{2,1,0:T(8,128)S(1)}, u32[]{:S(2)}, u32[]{:S(2)}) collective-permute-start(f32[3,10,512]{2,1,0:T(8,128)S(1)} %get-tuple-element.32), channel_id=1, source_target_pairs={{0,4},{4,8},{8,12},{12,16},{16,20},{20,24},{24,28},{28,32},{32,36}... | collective-permute-start | bytes 184328 | tf_op jit(solution)/shard_map/ppermute | solution.py:727
  23.2 4.9 %all-to-all-done = f32[64,1,384]{2,1,0:T(1,128)S(1)} async-done(((f32[64,1,384]{2,1,0:T(1,128)}), f32[64,1,384]{2,1,0:T(1,128)S(1)}, u32[]{:S(2)}, u32[]{:S(2)}) %all-to-all-start) | async-done | bytes 98336 | tf_op jit(solution)/shard_map/all_to_all | solution.py:734
  28.2 0.0 copy-start.4
  28.2 0.6 copy-done.4
  28.8 3.1 %shard_map.104 = (f32[1,3,16,512]{3,2,1,0:T(8,128)}, f32[3,10,512]{2,1,0:T(8,128)S(1)}, f32[3,10,512]{2,1,0:T(8,128)S(1)}, f32[152,128]{1,0:T(8,128)S(1)}, f32[3...) custom-call(f32[64,384]{1,0:T(8,128)S(1)} %bitcast.15, ...), custom_call_target="tpu_custom_call" | custom-call | tf_op jit(solution)/shard_map/pallas_call | solution.py:745
  32.0 2.4 %collective-permute-start = (f32[3,10,512]{2,1,0:T(8,128)S(1)}, f32[3,10,512]{2,1,0:T(8,128)S(1)}, u32[]{:S(2)}, u32[]{:S(2)}) collective-permute-start(f32[3,10,512]{2,1,0:T(8,128)S(1)} %get-tuple-element.18), channel_id=1, source_target_pairs={{0,4},{4,8},{8,12},{12,16},{16,20},{20,24},{24,28},{28,32},{32,36}... | collective-permute-start | bytes 184328 | tf_op jit(solution)/shard_map/ppermute | solution.py:759
  34.4 0.0 copy-start.3
  34.4 2.1 %collective-permute-start.1 = (f32[3,10,512]{2,1,0:T(8,128)S(1)}, f32[3,10,512]{2,1,0:T(8,128)S(1)}, u32[]{:S(2)}, u32[]{:S(2)}) collective-permute-start(f32[3,10,512]{2,1,0:T(8,128)S(1)} %get-tuple-element.19), channel_id=1, source_target_pairs={{4,0},{8,4},{12,8},{16,12},{20,16},{24,20},{28,24},{32,28},{36,32}... | collective-permute-start | bytes 184328 | tf_op jit(solution)/shard_map/ppermute | solution.py:760
  36.5 0.0 collective-permute-done.3.after
  36.5 0.0 collective-permute-done.2.before
  36.5 1.9 %shard_map.105 = (f32[3,4,48,128]{3,2,1,0:T(8,128)S(1)}, f32[3,4,32,128]{3,2,1,0:T(8,128)S(1)}, f32[3,4,32,128]{3,2,1,0:T(8,128)S(1)}, s32[32,128]{1,0:T(8,128)S(1)}) custom-call(f32[1,3,16,512]{3,2,1,0:T(8,128)S(1)} %copy-done.2, f32[3,10,512]{2,1,0:T(8,128)S(1)} %collective-permute-done.2.before, f32[3,10,512]{2,1,0:T(8,128)S(1)} %collective-permute-done.3.after, ...), custom_call_target="tpu_custom_call" | custom-call | tf_op jit(solution)/shard_map/pallas_call | solution.py:735
  38.3 0.0 collective-permute-done.before_strip
  38.4 2.1 %collective-permute-done.1.after_strip = f32[3,10,512]{2,1,0:T(8,128)S(1)} collective-permute-done((f32[3,10,512]{2,1,0:T(8,128)S(1)}, f32[3,10,512]{2,1,0:T(8,128)S(1)}, u32[]{:S(2)}, u32[]{:S(2)}) %collective-permute-start.1) | collective-permute-done | bytes 61472 | tf_op jit(solution)/shard_map/ppermute | solution.py:760
  40.5 6.4 %shard_map.106 = f32[64,384]{1,0:T(8,128)S(1)} custom-call(f32[1,3,16,512]{3,2,1,0:T(8,128)S(1)} %copy-done.3, f32[3,10,512]{2,1,0:T(8,128)S(1)} %collective-permute-done.before_strip, f32[3,10,512]{2,1,0:T(8,128)S(1)} %collective-permute-done.1.after_strip, f32[3,4,48,128]{3,2,1,0:T(8,128)S(1)} %get-tuple-element.20.ext_ref, ...), custom_call_target="tpu_custom_call" | custom-call | tf_op jit(solution)/shard_map/pallas_call | solution.py:761
  46.9 0.0 copy-start.1
  46.9 0.1 copy.16
  47.0 19.3 %all_to_all.22 = f32[64,1,384]{2,1,0:T(1,128)S(1)} all-to-all(f32[64,1,384]{2,1,0:T(1,128)S(1)} %copy.16), channel_id=1, replica_groups=mesh['space'=64,'view'=4] {'space'}, dimensions={0} | all-to-all | bytes 196608 | tf_op jit(solution)/shard_map/all_to_all | solution.py:791
  66.3 1.0 %shard_map.107 = (f32[152,128]{1,0:T(8,128)S(1)}, f32[1,128]{1,0:T(1,128)}) custom-call(f32[64,384]{1,0:T(8,128)S(1)} %bitcast.16, s32[32,128]{1,0:T(8,128)S(1)} %get-tuple-element.28.inv_ref, f32[1,3]{1,0:T(1,128)S(1)} %copy-done.5), custom_call_target="tpu_custom_call" | custom-call | tf_op jit(solution)/shard_map/pallas_call | solution.py:792
  67.3 2.5 %collective-permute-start.6 = (f32[152,128]{1,0:T(8,128)S(1)}, f32[152,128]{1,0:T(8,128)S(1)}, u32[]{:S(2)}, u32[]{:S(2)}) collective-permute-start(f32[152,128]{1,0:T(8,128)S(1)} %get-tuple-element.29.rec0), channel_id=1, source_target_pairs={{0,3},{1,0},{2,1},{3,2},{4,7},{5,4},{6,5},{7,6},{8,11},{9,8},{10,9... | collective-permute-start | bytes 233480 | tf_op jit(solution)/shard_map/ppermute | solution.py:798
  69.8 0.5 collective-permute-start.5
  70.3 0.6 collective-permute-start.4
  70.9 0.3 collective-permute-done.6.rec3
  71.3 3.4 %collective-permute-done.5.rec2 = f32[152,128]{1,0:T(8,128)S(1)} collective-permute-done((f32[152,128]{1,0:T(8,128)S(1)}, f32[152,128]{1,0:T(8,128)S(1)}, u32[]{:S(2)}, u32[]{:S(2)}) %collective-permute-start.5) | collective-permute-done | bytes 77856 | tf_op jit(solution)/shard_map/ppermute | solution.py:798
  74.6 2.1 %collective-permute-done.4.rec1 = f32[152,128]{1,0:T(8,128)S(1)} collective-permute-done((f32[152,128]{1,0:T(8,128)S(1)}, f32[152,128]{1,0:T(8,128)S(1)}, u32[]{:S(2)}, u32[]{:S(2)}) %collective-permute-start.4) | collective-permute-done | bytes 77856 | tf_op jit(solution)/shard_map/ppermute | solution.py:798
  76.7 1.4 %shard_map.108 = f32[59,2048]{1,0:T(8,128)} custom-call(f32[59,2048]{1,0:T(8,128)S(1)} %copy-done.1, f32[152,128]{1,0:T(8,128)S(1)} %get-tuple-element.29.rec0, f32[152,128]{1,0:T(8,128)S(1)} %collective-permute-done.4.rec1, f32[152,128]{1,0:T(8,128)S(1)} %collective-permute-done.5.rec2, f32[152,128]{1,0:T(8,128)S(1)} %collective-permute-done.6.rec3), custom_call_target="tpu_custom_call" | custom-call | tf_op jit(solution)/shard_map/pallas_call | solution.py:801
  (15 shorter events, 0.1 us)
Async XLA Ops:
  0.6 0.9 %copy-start.5 = (f32[1,3]{1,0:T(1,128)S(1)}, f32[1,3]{1,0:T(1,128)}, u32[]{:S(2)}) copy-start(f32[1,3]{1,0:T(1,128)} %cam_ref.3) | copy-start | bytes 40
  0.6 0.9 %copy-start.8 = (s32[1,64]{1,0:T(1,128)S(1)}, s32[1,64]{1,0:T(1,128)}, u32[]{:S(2)}) copy-start(s32[1,64]{1,0:T(1,128)} %rank_ref.1) | copy-start | bytes 772
  0.7 0.9 %copy-start.7 = (s32[1,64]{1,0:T(1,128)S(1)}, s32[1,64]{1,0:T(1,128)}, u32[]{:S(2)}) copy-start(s32[1,64]{1,0:T(1,128)} %cnt_ref.1) | copy-start | bytes 772
  0.7 0.9 %copy-start.6 = (s32[1,128]{1,0:T(1,128)S(1)}, s32[1,128]{1,0:T(1,128)}, u32[]{:S(2)}) copy-start(s32[1,128]{1,0:T(1,128)} %blk_ref.1) | copy-start | bytes 1540
  1.5 1.0 %copy-start = (f32[59,2048]{1,0:T(8,128)S(1)}, f32[59,2048]{1,0:T(8,128)}, u32[]{:S(2)}) copy-start(f32[59,2048]{1,0:T(8,128)} %p_ref.3) | copy-start | bytes 1449988
  4.3 13.3 %copy-start.2 = (f32[1,3,16,512]{3,2,1,0:T(8,128)S(1)}, f32[1,3,16,512]{3,2,1,0:T(8,128)}, u32[]{:S(2)}) copy-start(f32[1,3,16,512]{3,2,1,0:T(8,128)} %own.1) | copy-start | bytes 294916
  4.3 23.9 %all-to-all-start = ((f32[64,1,384]{2,1,0:T(1,128)}), f32[64,1,384]{2,1,0:T(1,128)S(1)}, u32[]{:S(2)}, u32[]{:S(2)}) async-start(f32[64,1,384]{2,1,0:T(1,128)} %copy.14), calls=%async_computation | async-start | bytes 196608 | tf_op jit(solution)/shard_map/all_to_all | solution.py:734
  17.6 18.8 %collective-permute-start.3 = (f32[3,10,512]{2,1,0:T(8,128)S(1)}, f32[3,10,512]{2,1,0:T(8,128)S(1)}, u32[]{:S(2)}, u32[]{:S(2)}) collective-permute-start(f32[3,10,512]{2,1,0:T(8,128)S(1)} %get-tuple-element.31), channel_id=1, source_target_pairs={{4,0},{8,4},{12,8},{16,12},{20,16},{24,20},{28,24},{32,28},{36,32}... | collective-permute-start | bytes 184328 | tf_op jit(solution)/shard_map/ppermute | solution.py:728
  20.0 16.4 %collective-permute-start.2 = (f32[3,10,512]{2,1,0:T(8,128)S(1)}, f32[3,10,512]{2,1,0:T(8,128)S(1)}, u32[]{:S(2)}, u32[]{:S(2)}) collective-permute-start(f32[3,10,512]{2,1,0:T(8,128)S(1)} %get-tuple-element.32), channel_id=1, source_target_pairs={{0,4},{4,8},{8,12},{12,16},{16,20},{20,24},{24,28},{28,32},{32,36}... | collective-permute-start | bytes 184328 | tf_op jit(solution)/shard_map/ppermute | solution.py:727
  28.2 0.7 copy-start.4
  32.0 6.4 %collective-permute-start = (f32[3,10,512]{2,1,0:T(8,128)S(1)}, f32[3,10,512]{2,1,0:T(8,128)S(1)}, u32[]{:S(2)}, u32[]{:S(2)}) collective-permute-start(f32[3,10,512]{2,1,0:T(8,128)S(1)} %get-tuple-element.18), channel_id=1, source_target_pairs={{0,4},{4,8},{8,12},{12,16},{16,20},{20,24},{24,28},{28,32},{32,36}... | collective-permute-start | bytes 184328 | tf_op jit(solution)/shard_map/ppermute | solution.py:759
  34.4 6.1 %copy-start.3 = (f32[1,3,16,512]{3,2,1,0:T(8,128)S(1)}, f32[1,3,16,512]{3,2,1,0:T(8,128)}, u32[]{:S(2)}) copy-start(f32[1,3,16,512]{3,2,1,0:T(8,128)} %get-tuple-element.15.strip_ref) | copy-start | bytes 294916
  34.4 6.1 %collective-permute-start.1 = (f32[3,10,512]{2,1,0:T(8,128)S(1)}, f32[3,10,512]{2,1,0:T(8,128)S(1)}, u32[]{:S(2)}, u32[]{:S(2)}) collective-permute-start(f32[3,10,512]{2,1,0:T(8,128)S(1)} %get-tuple-element.19), channel_id=1, source_target_pairs={{4,0},{8,4},{12,8},{16,12},{20,16},{24,20},{28,24},{32,28},{36,32}... | collective-permute-start | bytes 184328 | tf_op jit(solution)/shard_map/ppermute | solution.py:760
  46.9 29.9 %copy-start.1 = (f32[59,2048]{1,0:T(8,128)S(1)}, f32[59,2048]{1,0:T(8,128)}, u32[]{:S(2)}) copy-start(f32[59,2048]{1,0:T(8,128)} %p_ref.3) | copy-start | bytes 1449988
  67.3 3.9 %collective-permute-start.6 = (f32[152,128]{1,0:T(8,128)S(1)}, f32[152,128]{1,0:T(8,128)S(1)}, u32[]{:S(2)}, u32[]{:S(2)}) collective-permute-start(f32[152,128]{1,0:T(8,128)S(1)} %get-tuple-element.29.rec0), channel_id=1, source_target_pairs={{0,3},{1,0},{2,1},{3,2},{4,7},{5,4},{6,5},{7,6},{8,11},{9,8},{10,9... | collective-permute-start | bytes 233480 | tf_op jit(solution)/shard_map/ppermute | solution.py:798
  69.8 4.8 %collective-permute-start.5 = (f32[152,128]{1,0:T(8,128)S(1)}, f32[152,128]{1,0:T(8,128)S(1)}, u32[]{:S(2)}, u32[]{:S(2)}) collective-permute-start(f32[152,128]{1,0:T(8,128)S(1)} %get-tuple-element.29.rec0), channel_id=1, source_target_pairs={{0,2},{1,3},{2,0},{3,1},{4,6},{5,7},{6,4},{7,5},{8,10},{9,11},{10,... | collective-permute-start | bytes 233480 | tf_op jit(solution)/shard_map/ppermute | solution.py:798
  70.3 6.4 %collective-permute-start.4 = (f32[152,128]{1,0:T(8,128)S(1)}, f32[152,128]{1,0:T(8,128)S(1)}, u32[]{:S(2)}, u32[]{:S(2)}) collective-permute-start(f32[152,128]{1,0:T(8,128)S(1)} %get-tuple-element.29.rec0), channel_id=1, source_target_pairs={{0,1},{1,2},{2,3},{3,0},{4,5},{5,6},{6,7},{7,4},{8,9},{9,10},{10,1... | collective-permute-start | bytes 233480 | tf_op jit(solution)/shard_map/ppermute | solution.py:798
where the time goes:
time: 78.6 us; the launch traced here: 78.2 us
  starting transfers between devices  26.9 us (34%)
  blocking collectives  19.3 us (25%)
  Pallas kernels  14.8 us (19%)
  waiting for transfers between devices  12.9 us (16%)
  local copies, waits for them, and re-layouts  3.41 us (4%)
  between operations  0.84 us (1%)
    all_to_all x1, blocking collectives, shards(): returned = lax.all_to_all(reply, 'space', 0, 0, tiled=True)  19.3 us
    all_to_all x1, starting transfers between devices, shards(): received = lax.all_to_all(message, 'space', 0, 0, tiled=True)  13.3 us
    pallas_call x1, Pallas kernels, shards(): call(loss_kernel, [((64, 384), F32)], [((CHUNKS, 48, LANES), F32), ((2, C...  6.41 us
    ppermute x3, waiting for transfers between devices, shards(): lax.ppermute(record_grads, 'view', [(i, (i + d) % views) for i in range(v...  5.8 us
    all_to_all x1, waiting for transfers between devices, shards(): received = lax.all_to_all(message, 'space', 0, 0, tiled=True)  4.95 us
    ppermute x3, starting transfers between devices, shards(): lax.ppermute(record_grads, 'view', [(i, (i + d) % views) for i in range(v...  3.6 us
    ppermute x1, starting transfers between devices, shards(): goal_before = lax.ppermute(target[0, :, 6:16], 'space', up)  3.2 us
    pallas_call x1, Pallas kernels, shards(): call(blend_kernel, [((1, 3, 16, 512), F32), ((3, 10, 512), F32), ((3, 10,...  3.14 us
  transfers between devices with their start and end apart: 8, of which 5 were waited for; matrix products, arithmetic and copies ran while one was open for 0% of the time, Pallas kernels for 6%

commit v1 on v0

--- a/solution.py
+++ b/solution.py
@@ -93,7 +93,7 @@
 
 
 def camera_values(rows):
-    angles = [jnp.broadcast_to(rows[i : i + 1, :], (8, LANES)) for i in range(3)]
+    angles = [jnp.broadcast_to(row, (8, LANES)) for row in rows]
     turn = turn_of(angles)
     basis = harmonics(turn[2])
     cell = lambda value: value[0:1, 0:1]
@@ -133,7 +133,7 @@
 
 
 def slot_lists(vis_ref):
-    natural = vis_ref[0].T
+    natural = vis_ref[...]
     lane = iota((K, LANES), 1)
     order = (lane % 64) * 2 + lane // 64
     return jnp.take_along_axis(natural, order, axis=1), order
@@ -144,9 +144,9 @@
     rest = jnp.concatenate(
         [table[LANES:TABLE, :], jnp.zeros((2 * LANES - TABLE, LANES), F32)], axis=0
     ).T
-    out_ref[:, 0:LANES] = first[0:64]
-    out_ref[:, LANES : 2 * LANES] = first[64:128]
-    out_ref[:, 2 * LANES : 3 * LANES] = rest[0:64] + pltpu.roll(rest[64:128], 64, 1)
+    out_ref[:, 0, 0:LANES] = first[0:64]
+    out_ref[:, 0, LANES : 2 * LANES] = first[64:128]
+    out_ref[:, 0, 2 * LANES : 3 * LANES] = rest[0:64] + pltpu.roll(rest[64:128], 64, 1)
 
 
 def from_message(in_ref):
@@ -156,16 +156,49 @@
     return first, rest.T, rest
 
 
-def send_kernel(p_ref, cam_ref, vis_ref, blk_ref, cnt_ref, rank_ref, out_ref, par, rec):
+def send_kernel(
+    p_hbm,
+    cam_hbm,
+    vis_hbm,
+    blk_hbm,
+    cnt_hbm,
+    rank_hbm,
+    bg_hbm,
+    out_ref,
+    p_ref,
+    cam_ref,
+    vis_ref,
+    blk_ref,
+    cnt_ref,
+    rank_ref,
+    bg_ref,
+    par,
+    rec,
+    sems,
+):
     me = lax.axis_index("space")
+    copies = [
+        pltpu.make_async_copy(source, target, sems.at[i])
+        for i, (source, target) in enumerate(
+            (
+                (p_hbm, p_ref),
+                (cam_hbm, cam_ref),
+                (vis_hbm, vis_ref),
+                (blk_hbm, blk_ref),
+                (cnt_hbm, cnt_ref),
+                (rank_hbm, rank_ref),
+                (bg_hbm, bg_ref),
+            )
+        )
+    ]
+    for copy in copies:
+        copy.start()
+    for copy in copies:
+        copy.wait()
     load_params(p_ref, par)
-    cam = jnp.broadcast_to(cam_ref[...], (8, 3))
-    rows = jnp.concatenate(
-        [jnp.broadcast_to(cam[0:1, i : i + 1], (1, LANES)) for i in range(3)]
-        + [jnp.zeros((5, LANES), F32)],
-        axis=0,
-    )
-    turn, basis = camera_values(rows)
+    spread = lambda ref: [jnp.broadcast_to(ref[0:1, i : i + 1], (1, LANES)) for i in range(3)]
+    angles = spread(cam_ref)
+    turn, basis = camera_values(angles)
     get = lambda index: dense_row(par, index)
     scales = [jnp.exp(get(3 + i)) for i in range(3)]
     quaternion, _ = unit([get(6 + i) for i in range(4)])
@@ -207,68 +240,65 @@
         channels.append(value)
     blk = jnp.take_along_axis(jnp.broadcast_to(blk_ref[...], (8, LANES)), order[0:8], axis=1)
     counts = jnp.concatenate([cnt_ref[...], cnt_ref[...]], axis=1)
-    ids = jnp.where(iota((8, LANES), 1) // 64 < counts, blk, -1).astype(F32)
+    ids = jnp.where(iota((1, LANES), 1) // 64 < counts, blk[0:1], -1).astype(F32)
     rank = jnp.sum(
         jnp.where(iota((1, 64), 1) == me, rank_ref[...], 0).astype(F32), axis=1, keepdims=True
     )
-    meta = jnp.where(iota((8, LANES), 0) == 0, ids, jnp.broadcast_to(rank, (8, LANES)))
-    to_message(out_ref, jnp.concatenate(channels + [meta], axis=0))
-
-
-def shift_right(chunks, amount, lane):
-    turned = [pltpu.roll(x, amount, 1) for x in chunks]
-    return [
-        jnp.where(lane < amount, turned[j - 1] if j else 0.0, turned[j]) for j in range(CHUNKS)
-    ]
-
-
-def shift_left(chunks, amount, lane):
-    turned = [pltpu.roll(x, LANES - amount, 1) for x in chunks]
-    return [
-        jnp.where(lane >= LANES - amount, turned[j + 1] if j < CHUNKS - 1 else 0.0, turned[j])
-        for j in range(CHUNKS)
-    ]
+    meta = [ids, jnp.broadcast_to(rank, (1, LANES))] + spread(bg_ref) + angles
+    to_message(out_ref, jnp.concatenate(channels + meta, axis=0))
 
 
 def across(chunks):
     lane = iota(chunks[0].shape, 1)
     total = [TAPS[5] * x for x in chunks]
     for s in range(1, 6):
-        right = shift_right(chunks, s, lane)
-        left = shift_left(chunks, s, lane)
-        total = [t + TAPS[5 + s] * (a + b) for t, a, b in zip(total, right, left)]
+        right = [pltpu.roll(x, s, 1) for x in chunks]
+        left = [pltpu.roll(x, LANES - s, 1) for x in chunks]
+        low, high = lane < s, lane >= LANES - s
+        before = [0.0] + right[:-1]
+        after = left[1:] + [0.0]
+        total = [
+            t + TAPS[5 + s] * (jnp.where(low, b, r) + jnp.where(high, a, f))
+            for t, b, r, f, a in zip(total, before, right, left, after)
+        ]
     return total
 
 
-def down(load, start, count):
-    total = TAPS[5] * load(start + 5, count)
-    for s in range(1, 6):
-        total = total + TAPS[5 + s] * (load(start + 5 - s, count) + load(start + 5 + s, count))
-    return total
-
-
-def fill_rows(ext, own, before, after, ch):
+def blur(source, start, count=8):
+    chunks = []
+    for j in range(CHUNKS):
+        load = lambda first: source[j, first : first + count, :]
+        total = TAPS[5] * load(start + 5)
+        for s in range(1, 6):
+            total = total + TAPS[5 + s] * (load(start + 5 - s) + load(start + 5 + s))
+        chunks.append(total)
+    return across(chunks)
+
+
+def fill_rows(ext, own, chip, next_chip, ch, even):
     for j in range(CHUNKS):
         cols = slice(j * LANES, (j + 1) * LANES)
         ext[j, 0:8, :] = jnp.zeros((8, LANES), F32)
         ext[j, 40:48, :] = jnp.zeros((8, LANES), F32)
-        ext[j, 6:16, :] = before[ch, :, cols]
+        near, far = chip[ch, :, cols], next_chip[ch, :, cols]
+        ext[j, 6:16, :] = jnp.where(even, far, near)
         ext[j, 16:32, :] = own[0, ch, :, cols]
-        ext[j, 32:42, :] = after[ch, :, cols]
-
-
-def target_kernel(own, before, after, vis_ref, ext_ref, mean_ref, square_ref, inv_ref, tmp, sq):
+        ext[j, 32:42, :] = jnp.where(even, near, far)
+
+
+def target_kernel(own, chip, next_chip, vis_ref, ext_ref, mean_ref, square_ref, inv_ref, tmp, sq):
+    even = lax.axis_index("space") % 2 == 0
+
     def channel(ch, carry):
-        fill_rows(tmp, own, before, after, ch)
+        fill_rows(tmp, own, chip, next_chip, ch, even)
         for j in range(CHUNKS):
             ext_ref[ch, j] = tmp[j]
             sq[j] = tmp[j] * tmp[j]
         for source, out in ((tmp, mean_ref), (sq, square_ref)):
-            blurred = across(
-                [down(lambda s, n: source[j, pl.ds(s, n), :], 6, 32) for j in range(CHUNKS)]
-            )
-            for j in range(CHUNKS):
-                out[ch, j] = blurred[j]
+            for top in range(0, 32, 8):
+                blurred = blur(source, 6 + top)
+                for j in range(CHUNKS):
+                    out[ch, j, top : top + 8, :] = blurred[j]
         return carry
 
     lax.fori_loop(0, 3, channel, 0)
@@ -322,15 +352,17 @@
 
 def blend_kernel(
     recv_ref,
-    bg_ref,
     strip_ref,
-    top_ref,
-    bottom_ref,
+    chip_ref,
+    next_ref,
     rec,
     colour_ref,
     before_ref,
     total_ref,
     nearer_ref,
+    through_ref,
+    alphas,
+    weights,
     logs,
     blocks_ref,
 ):
@@ -356,6 +388,8 @@
                     dx = dx0 + float(i)
                     alpha = opacity * jnp.exp((ma * dx - mb_y) * dx + mc_yy)
                     weight = alpha * through[i]
+                    alphas[k, g * GROUP + i] = alpha
+                    weights[k, g * GROUP + i] = weight
                     keep = 1.0 - alpha
                     through = through[:i] + (through[i] * keep,) + through[i + 1 :]
                     part[i] = part[i] * keep
@@ -368,7 +402,7 @@
             return through, log_sum, colours
 
         zero = jnp.zeros((8, LANES), F32)
-        _, log_sum, colours = lax.fori_loop(
+        through, log_sum, colours = lax.fori_loop(
             0,
             4,
             four,
@@ -381,6 +415,7 @@
         for i in range(GROUP):
             rows = pl.ds(pl.multiple_of((g * GROUP + i) * 8, 8), 8)
             logs[rows, :] = log_sum[i]
+            through_ref[rows, :] = through[i]
             for c in range(3):
                 colour_ref[c, rows, :] = colours[i][c]
         return carry
@@ -393,7 +428,7 @@
     live = id_row >= 0.0
     same = jnp.where((id_row == id_col) & live, 1.0, 0.0)
     nearer = jnp.where(rank_col < rank_row, same, 0.0).astype(BF16)
-    member = jnp.where(id_col == iota((LANES, LANES), 1).astype(F32), 1.0, 0.0).astype(BF16)
+    member = jnp.where(id_col == (iota((LANES, LANES), 1) % 64).astype(F32), 1.0, 0.0).astype(BF16)
     nearer_ref[...] = nearer
     log_all = logs[...]
     ahead = dot_mask(
@@ -405,119 +440,139 @@
     open_sky = jnp.exp(ahead[:, 2 * LANES : 3 * LANES])
     lane = iota((8, LANES), 1)
     for c in range(3):
-        back = bg_ref[0:1, c : c + 1]
-        blocks_ref[c] = dot_mask(before * colour_ref[c], member, 0) + back * open_sky
+        blocks_ref[c] = dot_mask(before * colour_ref[c], member, 0) + rest_rows[18 + c : 19 + c] * open_sky
+    pair = lane % 16 // 2
     for c in range(3):
-        for br in range(2):
-            for t in range(CHUNKS):
-                index = br * 32 + 8 * t + lane // 16
-                value = jnp.zeros((8, LANES), F32)
-                for cc in range(16):
-                    got = jnp.take_along_axis(blocks_ref[c, cc * 8 : cc * 8 + 8, :], index, axis=1)
-                    value = jnp.where(lane % 16 == cc, got, value)
-                strip_ref[0, c, br * 8 : br * 8 + 8, t * LANES : (t + 1) * LANES] = value
-    top_ref[...] = strip_ref[0, :, 0:10, :]
-    bottom_ref[...] = strip_ref[0, :, 6:16, :]
+        for p in range(8):
+            blocks_ref[c, p * 16 : p * 16 + 8, :] = jnp.where(
+                lane < 64,
+                blocks_ref[c, p * 16 : p * 16 + 8, :],
+                blocks_ref[c, p * 16 + 8 : p * 16 + 16, :],
+            )
+    for br in range(2):
+        for t in range(CHUNKS):
+            index = lane % 2 * 64 + (br * 32 + 8 * t) + lane // 16
+            values = [None] * 3
+            for p in range(8):
+                for c in range(3):
+                    got = jnp.take_along_axis(
+                        blocks_ref[c, p * 16 : p * 16 + 8, :], index, axis=1
+                    )
+                    values[c] = jnp.where(pair == p, got, values[c]) if p else got
+            for c in range(3):
+                strip_ref[0, c, br * 8 : br * 8 + 8, t * LANES : (t + 1) * LANES] = values[c]
+    even = me % 2 == 0
+    top = strip_ref[0, :, 0:10, :]
+    bottom = strip_ref[0, :, 6:16, :]
+    chip_ref[...] = jnp.where(even, bottom, top)
+    next_ref[...] = jnp.where(even, top, bottom)
 
 
 def loss_kernel(
     strip_ref,
-    before_strip,
-    after_strip,
+    chip,
+    next_chip,
     ext_ref,
     mean_ref,
     square_ref,
-    bg_ref,
     rec,
     colour_ref,
     before_ref,
     total_ref,
     nearer_ref,
+    through_ref,
+    alphas,
+    weights,
     out_ref,
     ext,
     prod,
     stat,
     grads,
+    spread_grads,
     pulled,
     cot,
-    log_cot,
-    alphas,
-    throughs,
+    behind_cot,
     sums,
     table,
 ):
     me = lax.axis_index("space")
-    t_row = iota((32, LANES), 0)
-    where = me * 16 - 5 + t_row
-    inside = jnp.where((where >= 0) & (where < 1024) & (t_row < 26), -0.2, 0.0)
-    own = (t_row >= 5) & (t_row < 21)
     first_c, second_c = SSIM_FIRST, SSIM_SECOND
+    even = me % 2 == 0
 
     def channel(ch, loss):
-        fill_rows(ext, strip_ref, before_strip, after_strip, ch)
+        fill_rows(ext, strip_ref, chip, next_chip, ch, even)
         for j in range(CHUNKS):
             a = ext[j]
             prod[0, j] = a * a
             prod[1, j] = a * ext_ref[ch, j]
-        blurred = []
-        for source in (ext, prod.at[0], prod.at[1]):
-            blurred.append(
-                across([down(lambda s, n: source[j, pl.ds(s, n), :], 6, 32) for j in range(CHUNKS)])
-            )
-        for j in range(CHUNKS):
-            ma, mb = blurred[0][j], mean_ref[ch, j]
-            mab = ma * mb
-            squares = ma * ma + mb * mb
-            n1 = 2.0 * mab + first_c
-            n2 = 2.0 * (blurred[2][j] - mab) + second_c
-            d1 = squares + first_c
-            d2 = (blurred[1][j] + square_ref[ch, j]) - squares + second_c
-            inverse = 1.0 / (d1 * d2)
-            ssim = n1 * n2 * inverse
-            loss = loss + jnp.where(own, 0.2 - 0.2 * ssim, 0.0)
-            seed = inside * inverse
-            g1 = seed * n2
-            g2 = seed * n1
-            scaled = inside * ssim
-            gd1 = scaled * inverse * d2
-            gd2 = scaled * inverse * d1
-            stat[0, j] = 2.0 * (mb * (g1 - g2) + ma * (gd2 - gd1))
-            stat[1, j] = -gd2
-            stat[2, j] = 2.0 * g2
-        spread = []
-        for q in range(3):
-            spread.append(
-                across([down(lambda s, n: stat[q, j, pl.ds(s, n), :], 0, 16) for j in range(CHUNKS)])
-            )
-        for j in range(CHUNKS):
-            a = ext[j, 16:32, :]
-            b = ext_ref[ch, j, 16:32, :]
-            differ = a - b
-            root = jnp.sqrt(differ * differ + SMOOTHING)
-            loss = loss + jnp.concatenate([0.8 * root, jnp.zeros((16, LANES), F32)], axis=0)
-            grads[ch, j] = (
-                spread[0][j] + 2.0 * a * spread[1][j] + b * spread[2][j] + 0.8 * differ / root
-            )
+        for top in range(0, 32, 8):
+            t_row = iota((8, LANES), 0) + top
+            where = me * 16 - 5 + t_row
+            inside = jnp.where((where >= 0) & (where < 1024) & (t_row < 26), -0.2, 0.0)
+            own = (t_row >= 5) & (t_row < 21)
+            blurred = [blur(source, 6 + top) for source in (ext, prod.at[0], prod.at[1])]
+            rows = slice(top, top + 8)
+            for j in range(CHUNKS):
+                ma, mb = blurred[0][j], mean_ref[ch, j, rows, :]
+                mab = ma * mb
+                squares = ma * ma + mb * mb
+                n1 = 2.0 * mab + first_c
+                n2 = 2.0 * (blurred[2][j] - mab) + second_c
+                d1 = squares + first_c
+                d2 = (blurred[1][j] + square_ref[ch, j, rows, :]) - squares + second_c
+                inverse = 1.0 / (d1 * d2)
+                ssim = n1 * n2 * inverse
+                loss = loss + jnp.where(own, 0.2 - 0.2 * ssim, 0.0)
+                seed = inside * inverse
+                g1 = seed * n2
+                g2 = seed * n1
+                scaled = seed * ssim
+                gd1 = scaled * d2
+                gd2 = scaled * d1
+                stat[0, j, rows, :] = 2.0 * (mb * (g1 - g2) + ma * (gd2 - gd1))
+                stat[1, j, rows, :] = -gd2
+                stat[2, j, rows, :] = 2.0 * g2
+        for top in (0, 8):
+            spread = [blur(stat.at[q], top) for q in range(3)]
+            rows = slice(16 + top, 24 + top)
+            for j in range(CHUNKS):
+                a = ext[j, rows, :]
+                b = ext_ref[ch, j, rows, :]
+                differ = a - b
+                root = jnp.sqrt(differ * differ + SMOOTHING)
+                loss = loss + 0.8 * root
+                grads[ch, j, top : top + 8, :] = (
+                    spread[0][j] + 2.0 * a * spread[1][j] + b * spread[2][j] + 0.8 * differ / root
+                )
         return loss
 
-    loss = lax.fori_loop(0, 3, channel, jnp.zeros((32, LANES), F32))
+    loss = jnp.zeros((8, LANES), F32)
+    for ch in range(3):
+        loss = channel(ch, loss)
     loss = jnp.sum(jnp.sum(loss, axis=0, keepdims=True), axis=1, keepdims=True)
 
     ids = row(rec[...], META, 8)
     live = ids >= 0.0
     block = jnp.maximum(ids, 0.0).astype(I32)
-    place = block // 8
-    start = block % 8 * 16
-    for c in range(3):
-        for cc in range(16):
-            value = jnp.zeros((8, LANES), F32)
-            for br in range(2):
-                for t in range(CHUNKS):
-                    got = jnp.take_along_axis(
-                        grads[c, t, br * 8 : br * 8 + 8, :], start + cc, axis=1
-                    )
-                    value = jnp.where(place == br * 4 + t, got, value)
-            pulled[c, cc * 8 : cc * 8 + 8, :] = jnp.where(live, value, 0.0)
+    lane = iota((8, LANES), 1)
+    place = lane % 64 // 8
+    for p in range(8):
+        start = lane % 8 * 16 + 2 * p + lane // 64
+        both = [None] * 3
+        for n in range(8):
+            br, t = divmod(n, CHUNKS)
+            for c in range(3):
+                got = jnp.take_along_axis(grads[c, t, br * 8 : br * 8 + 8, :], start, axis=1)
+                both[c] = jnp.where(place == n, got, both[c]) if n else got
+        for c in range(3):
+            spread_grads[c, p] = both[c]
+    for odd in range(2):
+        index = block + 64 * odd
+        for p in range(8):
+            for c in range(3):
+                value = jnp.take_along_axis(spread_grads[c, p], index, axis=1)
+                first = (2 * p + odd) * 8
+                pulled[c, first : first + 8, :] = jnp.where(live, value, 0.0)
     before = before_ref[...]
     behind = jnp.zeros((LANES, LANES), F32)
     sky = jnp.zeros((LANES, LANES), F32)
@@ -526,8 +581,11 @@
         scaled = before * g
         cot[c] = scaled
         behind = behind + scaled * colour_ref[c]
-        sky = sky + bg_ref[0:1, c : c + 1] * g
-    log_cot[...] = dot_mask(behind, nearer_ref[...], 1) + total_ref[...] * sky
+        sky = sky + rec[META + 2 + c : META + 3 + c, :] * g
+    log_cot = dot_mask(behind, nearer_ref[...], 1) + total_ref[...] * sky
+    left = through_ref[...]
+    some = left > 0.0
+    behind_cot[...] = jnp.where(some, log_cot / jnp.where(some, left, 1.0), 0.0)
 
     corner_x, corner_y = corners(ids, me)
     y_grid = corner_y + iota((8, LANES), 0).astype(F32)
@@ -535,17 +593,7 @@
     def group(g, carry):
         base = corner_x + (g * GROUP).astype(F32)
         rows = [pl.ds(pl.multiple_of((g * GROUP + i) * 8, 8), 8) for i in range(GROUP)]
-        through = [jnp.ones((8, LANES), F32)] * GROUP
-        for k in range(K):
-            dx0, dy, ma, mb_y, mc_yy, opacity = splat_terms(rec, k, base, y_grid)
-            for i in range(GROUP):
-                dx = dx0 + float(i)
-                alpha = opacity * jnp.exp((ma * dx - mb_y) * dx + mc_yy)
-                alphas[k, i] = alpha
-                throughs[k, i] = through[i]
-                through[i] = through[i] * (1.0 - alpha)
-
-        suffix = tuple(log_cot[rows[i], :] for i in range(GROUP))
+        suffix = tuple(behind_cot[rows[i], :] for i in range(GROUP))
         pull = [[cot[c, rows[i], :] for c in range(3)] for i in range(GROUP)]
         zero = jnp.zeros((8, LANES), F32)
 
@@ -559,15 +607,12 @@
             after = []
             for i in range(GROUP):
                 dx = dx0 + float(i)
-                alpha = alphas[k, i]
-                seen = throughs[k, i]
-                gain = seen * (
-                    pull[i][0] * tint[0] + pull[i][1] * tint[1] + pull[i][2] * tint[2]
+                weight = weights[k, g * GROUP + i]
+                gain = (
+                    pull[i][0] * tint[0] + pull[i][1] * tint[1] + pull[i][2] * tint[2] - suffix[i]
                 )
-                g_alpha = gain - suffix[i] / (1.0 - alpha)
-                after.append(suffix[i] + alpha * gain)
-                moment = alpha * g_alpha
-                weight = alpha * seen
+                after.append(suffix[i] + alphas[k, g * GROUP + i] * gain)
+                moment = weight * gain
                 shade = [shade[c] + weight * pull[i][c] for c in range(3)]
                 moment_x = moment * dx
                 s0 = s0 + moment
@@ -604,11 +649,13 @@
         return carry
 
     lax.fori_loop(0, K, finish, 0)
-    table[META:TABLE, :] = jnp.broadcast_to(loss, (8, LANES))
+    table[META:TABLE, :] = jnp.concatenate(
+        [jnp.broadcast_to(loss, (5, LANES)), rec[META + 5 : TABLE, :]], axis=0
+    )
     to_message(out_ref, table[...])
 
 
-def gather_kernel(recv_ref, inv_ref, cam_ref, out_ref, loss_ref, rec):
+def gather_kernel(recv_ref, inv_ref, out_ref, loss_ref, rec):
     first, rest_rows, rest_cols = from_message(recv_ref)
     rec[0:LANES, :] = first
     rec[LANES:META, :] = rest_rows[0:16]
@@ -620,11 +667,7 @@
             source = jnp.broadcast_to(rec[ch * K + k : ch * K + k + 1, :], (16, LANES))
             value = jnp.where(at_k == k, jnp.take_along_axis(source, at_slot, axis=1), value)
         out_ref[ch * 16 : ch * 16 + 16, :] = value
-    out_ref[META:TABLE, :] = jnp.concatenate(
-        [jnp.broadcast_to(cam_ref[0:1, i : i + 1], (1, LANES)) for i in range(3)]
-        + [jnp.zeros((5, LANES), F32)],
-        axis=0,
-    )
+    out_ref[META:TABLE, :] = rest_rows[16:24]
     total = jnp.sum(rest_cols[0:64, 16:17], axis=0, keepdims=True)
     loss_ref[...] = jnp.broadcast_to(total * (1.0 / 1572864.0), (1, LANES))
 
@@ -646,7 +689,7 @@
     g_colour = []
     bases = []
     for v in range(4):
-        turn, basis = camera_values(views[v, META:TABLE, :])
+        turn, basis = camera_values([views[v, META + 5 + i : META + 6 + i, :] for i in range(3)])
         bases.append(basis)
         g = [views[v, ch * 16 : ch * 16 + 16, :] for ch in range(9)]
         unscaled = [
@@ -708,30 +751,48 @@
             ]
 
 
-def call(kernel, outs, scratch=(), vmem=None):
+def call(kernel, outs, scratch=(), copied=0):
+    extra = {"in_specs": [pl.BlockSpec(memory_space=pltpu.HBM)] * copied} if copied else {}
+    sems = [pltpu.SemaphoreType.DMA((copied,))] if copied else []
     return pl.pallas_call(
         kernel,
         out_shape=[jax.ShapeDtypeStruct(shape, dtype) for shape, dtype in outs],
-        scratch_shapes=[pltpu.VMEM(shape, dtype) for shape, dtype in scratch],
-        compiler_params=pltpu.CompilerParams(vmem_limit_bytes=vmem or 16 << 20),
+        scratch_shapes=[pltpu.VMEM(shape, dtype) for shape, dtype in scratch] + sems,
+        compiler_params=pltpu.CompilerParams(vmem_limit_bytes=(60 if copied else 16) << 20),
+        **extra,
     )
 
 
 def shards(params, visible, blocks, counts, depth_rank, camera, background, target):
     devices = lax.axis_size("space")
     views = lax.axis_size("view")
-    up = [(i, i + 1) for i in range(devices - 1)]
-    below = [(i + 1, i) for i in range(devices - 1)]
+    chip = [(i, i ^ 1) for i in range(devices)]
+    next_chip = [(i, i + 1 if i % 2 else i - 1) for i in range(1, devices - 1)]
+    even = lax.axis_index("space") % 2 == 0
     tile = (LANES, LANES)
-
-    goal_before = lax.ppermute(target[0, :, 6:16], "space", up)
-    goal_after = lax.ppermute(target[0, :, 0:10], "space", below)
+    kept = ((K, 16, 8, LANES), F32)
+    lists = visible[0].T
+
+    goal_top, goal_bottom = target[0, :, 0:10], target[0, :, 6:16]
+    goal_chip = lax.ppermute(jnp.where(even, goal_bottom, goal_top), "space", chip)
+    goal_next = lax.ppermute(jnp.where(even, goal_top, goal_bottom), "space", next_chip)
     (message,) = call(
         send_kernel,
-        [((64, 384), F32)],
-        [((8, LANES, LANES), F32), ((META, LANES), F32)],
-    )(params, camera, visible, blocks, counts, depth_rank)
-    received = lax.all_to_all(message, "space", 0, 0, tiled=True)
+        [((64, 1, 384), F32)],
+        [
+            (params.shape, F32),
+            ((1, 3), F32),
+            ((K, LANES), I32),
+            ((1, LANES), I32),
+            ((1, 64), I32),
+            ((1, 64), I32),
+            ((1, 3), F32),
+            ((8, LANES, LANES), F32),
+            ((META, LANES), F32),
+        ],
+        copied=7,
+    )(params, camera, lists, blocks, counts, depth_rank, background)
+    received = lax.all_to_all(message, "space", 0, 0, tiled=True).reshape(64, 384)
     goal, goal_mean, goal_square, inverse = call(
         target_kernel,
         [
@@ -741,8 +802,8 @@
             ((32, LANES), I32),
         ],
         [((CHUNKS, 48, LANES), F32)] * 2,
-    )(target, goal_before, goal_after, visible)
-    strip, top, bottom, records, colours, before, total, nearer = call(
+    )(target, goal_chip, goal_next, lists)
+    strip, to_chip, to_next, records, colours, before, total, nearer, through, alphas, weights = call(
         blend_kernel,
         [
             ((1, 3, 16, 512), F32),
@@ -753,47 +814,51 @@
             (tile, F32),
             (tile, F32),
             (tile, BF16),
+            (tile, F32),
+            kept,
+            kept,
         ],
         [(tile, F32), ((3, *tile), F32)],
-    )(received, background)
-    strip_before = lax.ppermute(bottom, "space", up)
-    strip_after = lax.ppermute(top, "space", below)
+    )(received)
+    strip_chip = lax.ppermute(to_chip, "space", chip)
+    strip_next = lax.ppermute(to_next, "space", next_chip)
     (reply,) = call(
         loss_kernel,
-        [((64, 384), F32)],
+        [((64, 1, 384), F32)],
         [
             ((CHUNKS, 48, LANES), F32),
             ((2, CHUNKS, 48, LANES), F32),
             ((3, CHUNKS, 32, LANES), F32),
             ((3, CHUNKS, 16, LANES), F32),
+            ((3, 8, 8, LANES), F32),
             ((3, *tile), F32),
             ((3, *tile), F32),
             (tile, F32),
-            ((K, GROUP, 8, LANES), F32),
-            ((K, GROUP, 8, LANES), F32),
             ((K, 6, 8, LANES), F32),
             ((TABLE, LANES), F32),
         ],
     )(
         strip,
-        strip_before,
-        strip_after,
+        strip_chip,
+        strip_next,
         goal,
         goal_mean,
         goal_square,
-        background,
         records,
         colours,
         before,
         total,
         nearer,
+        through,
+        alphas,
+        weights,
     )
-    returned = lax.all_to_all(reply, "space", 0, 0, tiled=True)
+    returned = lax.all_to_all(reply, "space", 0, 0, tiled=True).reshape(64, 384)
     record_grads, loss = call(
         gather_kernel,
         [((TABLE, LANES), F32), ((1, LANES), F32)],
         [((META, LANES), F32)],
-    )(returned, inverse, camera)
+    )(returned, inverse)
     others = [
         lax.ppermute(record_grads, "view", [(i, (i + d) % views) for i in range(views)])
         for d in range(1, views)

time: 78.6 us -> 70.7 us (0.90)
  starting transfers between devices: 26.9 us -> 23.2 us
  local copies, waits for them, and re-layouts: 3.41 us -> 0.03 us
  blocking collectives: 19.3 us -> 17.3 us
  waiting for transfers between devices: 12.9 us -> 14.7 us
    ppermute x4, starting transfers between devices: 10 us -> 6.27 us  [the longest x1 3.54 us: shards(): lax.ppermute(jnp.where(even, goal_top, goal_bottom), 'space', next_chip)]
    unnamed x21 -> x10, local copies, waits for them, and re-layouts: 2.55 us -> 0.03 us
    all_to_all x1, blocking collectives: 19.3 us -> 17.3 us  [shards(): returned = lax.all_to_all(reply, 'space', 0, 0, tiled=True).reshape(64, 384)]
    all_to_all x1, waiting for transfers between devices: 4.95 us -> 6.86 us  [shards(): lax.all_to_all(message, 'space', 0, 0, tiled=True).reshape(64, 384)]
    all_to_all x2 -> x0, local copies, waits for them, and re-layouts: 0.85 us -> none  [the longest x1 0.74 us: shards(): received = lax.all_to_all(message, 'space', 0, 0, tiled=True)]
where the time goes in v1:
time: 70.7 us; the launch traced here: 70.4 us
  starting transfers between devices  23.2 us (33%)
  blocking collectives  17.3 us (24%)
  waiting for transfers between devices  14.7 us (21%)
  Pallas kernels  14.4 us (20%)
  between operations  0.77 us (1%)
    all_to_all x1, blocking collectives, shards(): returned = lax.all_to_all(reply, 'space', 0, 0, tiled=True).reshape(64, 384)  17.3 us
    all_to_all x1, starting transfers between devices, shards(): lax.all_to_all(message, 'space', 0, 0, tiled=True).reshape(64, 384)  13.3 us
    all_to_all x1, waiting for transfers between devices, shards(): lax.all_to_all(message, 'space', 0, 0, tiled=True).reshape(64, 384)  6.86 us
    ppermute x3, waiting for transfers between devices, shards(): lax.ppermute(record_grads, 'view', [(i, (i + d) % views) for i in range(v...  5.8 us
    pallas_call x1, Pallas kernels, shards(): call(loss_kernel, [((64, 1, 384), F32)], [((CHUNKS, 48, LANES), F32), ((2...  4.73 us
    ppermute x3, starting transfers between devices, shards(): lax.ppermute(record_grads, 'view', [(i, (i + d) % views) for i in range(v...  3.6 us
    ppermute x1, starting transfers between devices, shards(): lax.ppermute(jnp.where(even, goal_top, goal_bottom), 'space', next_chip)  3.54 us
    pallas_call x1, Pallas kernels, shards(): call(send_kernel, [((64, 1, 384), F32)], [(params.shape, F32), ((1, 3), F...  2.82 us
  transfers between devices with their start and end apart: 8, of which 5 were waited for; matrix products, arithmetic and copies ran while one was open for 0% of the time, Pallas kernels for 6%

profile of v1, /device:TPU:1, one launch (start us, length us, event | category | flops | bytes accessed | tf_op | source)
XLA Modules:
  0.0 70.4 jit_solution(1655768422862806446)
XLA Ops:
  0.6 2.8 %shard_map.103 = f32[64,1,384]{2,1,0:T(1,128)} custom-call(f32[59,2048]{1,0:T(8,128)} %p_ref.1, f32[1,3]{1,0:T(1,128)} %cam_hbm.1, s32[16,128]{1,0:T(8,128)} %bitcast.17, s32[1,128]{1,0:T(1,128)} %blk_hbm.1, s32[1,64]{1,0:T(1,128)} %cnt_hbm.1, s32[1,64]{1,0:T(1,128)} %rank_hbm.1, f32[1,3]{1,0:T(1,128)} %bg_hbm.1), custom_call_target="tpu_custom_call" | custom-call | tf_op jit(solution)/shard_map/pallas_call | solution.py:779
  3.5 0.0 copy-start.1
  3.5 13.3 %all-to-all-start = ((f32[64,1,384]{2,1,0:T(1,128)}), f32[64,1,384]{2,1,0:T(1,128)S(1)}, u32[]{:S(2)}, u32[]{:S(2)}) async-start(f32[64,1,384]{2,1,0:T(1,128)} %shard_map.103), calls=%async_computation | async-start | bytes 196608 | tf_op jit(solution)/shard_map/all_to_all | solution.py:795
  16.8 0.0 copy-done.1
  16.8 3.5 %collective-permute-start.3 = (f32[3,10,512]{2,1,0:T(8,128)S(1)}, f32[3,10,512]{2,1,0:T(8,128)S(1)}, u32[]{:S(2)}, u32[]{:S(2)}) collective-permute-start(f32[3,10,512]{2,1,0:T(8,128)S(1)} %get-tuple-element.37), channel_id=1, source_target_pairs={{4,8},{8,4},{12,16},{16,12},{20,24},{24,20},{28,32},{32,28},{36,40... | collective-permute-start | bytes 184328 | tf_op jit(solution)/shard_map/ppermute | solution.py:778
  20.4 0.1 collective-permute-start.2
  20.5 6.9 %all-to-all-done = f32[64,1,384]{2,1,0:T(1,128)S(1)} async-done(((f32[64,1,384]{2,1,0:T(1,128)}), f32[64,1,384]{2,1,0:T(1,128)S(1)}, u32[]{:S(2)}, u32[]{:S(2)}) %all-to-all-start) | async-done | bytes 98336 | tf_op jit(solution)/shard_map/all_to_all | solution.py:795
  27.3 0.0 copy-start.3
  27.4 2.7 %shard_map.104 = (f32[1,3,16,512]{3,2,1,0:T(8,128)}, f32[3,10,512]{2,1,0:T(8,128)S(1)}, f32[3,10,512]{2,1,0:T(8,128)S(1)}, f32[152,128]{1,0:T(8,128)S(1)}, f32[3...) custom-call(f32[64,384]{1,0:T(8,128)S(1)} %bitcast.15), custom_call_target="tpu_custom_call" | custom-call | tf_op jit(solution)/shard_map/pallas_call | solution.py:806
  30.1 0.4 collective-permute-start
  30.5 0.0 copy-start.2
  30.5 2.2 %collective-permute-start.1 = (f32[3,10,512]{2,1,0:T(8,128)S(1)}, f32[3,10,512]{2,1,0:T(8,128)S(1)}, u32[]{:S(2)}, u32[]{:S(2)}) collective-permute-start(f32[3,10,512]{2,1,0:T(8,128)S(1)} %get-tuple-element.22), channel_id=1, source_target_pairs={{4,8},{8,4},{12,16},{16,12},{20,24},{24,20},{28,32},{32,28},{36,40... | collective-permute-start | bytes 184328 | tf_op jit(solution)/shard_map/ppermute | solution.py:824
  32.7 0.0 collective-permute-done.3.next_chip
  32.7 0.0 collective-permute-done.2.chip
  32.7 0.0 copy-done.3
  32.8 1.8 %shard_map.105 = (f32[3,4,48,128]{3,2,1,0:T(8,128)S(1)}, f32[3,4,32,128]{3,2,1,0:T(8,128)S(1)}, f32[3,4,32,128]{3,2,1,0:T(8,128)S(1)}, s32[32,128]{1,0:T(8,128)S(1)}) custom-call(f32[1,3,16,512]{3,2,1,0:T(8,128)S(1)} %copy-done.1, f32[3,10,512]{2,1,0:T(8,128)S(1)} %collective-permute-done.2.chip, f32[3,10,512]{2,1,0:T(8,128)S(1)} %collective-permute-done.3.next_chip, ...), custom_call_target="tpu_custom_call" | custom-call | tf_op jit(solution)/shard_map/pallas_call | solution.py:796
  34.5 0.0 collective-permute-done.chip
  34.6 2.0 %collective-permute-done.1.next_chip = f32[3,10,512]{2,1,0:T(8,128)S(1)} collective-permute-done((f32[3,10,512]{2,1,0:T(8,128)S(1)}, f32[3,10,512]{2,1,0:T(8,128)S(1)}, u32[]{:S(2)}, u32[]{:S(2)}) %collective-permute-start.1) | collective-permute-done | bytes 61472 | tf_op jit(solution)/shard_map/ppermute | solution.py:824
  36.5 0.0 copy-done.2
  36.5 0.0 copy-start
  36.5 4.7 %shard_map.106 = f32[64,1,384]{2,1,0:T(1,128)S(1)} custom-call(f32[1,3,16,512]{3,2,1,0:T(8,128)S(1)} %copy-done.2, f32[3,10,512]{2,1,0:T(8,128)S(1)} %collective-permute-done.chip, f32[3,10,512]{2,1,0:T(8,128)S(1)} %collective-permute-done.1.next_chip, f32[3,4,48,128]{3,2,1,0:T(8,128)S(1)} %get-tuple-element.23.ext_ref, ...), custom_call_target="tpu_custom_call" | custom-call | tf_op jit(solution)/shard_map/pallas_call | solution.py:825
  41.3 17.3 %all_to_all.10 = f32[64,1,384]{2,1,0:T(1,128)S(1)} all-to-all(f32[64,1,384]{2,1,0:T(1,128)S(1)} %shard_map.106), channel_id=1, replica_groups=mesh['space'=64,'view'=4] {'space'}, dimensions={0} | all-to-all | bytes 196608 | tf_op jit(solution)/shard_map/all_to_all | solution.py:856
  58.6 1.0 %shard_map.107 = (f32[152,128]{1,0:T(8,128)S(1)}, f32[1,128]{1,0:T(1,128)}) custom-call(f32[64,384]{1,0:T(8,128)S(1)} %bitcast.16, s32[32,128]{1,0:T(8,128)S(1)} %get-tuple-element.34.inv_ref), custom_call_target="tpu_custom_call" | custom-call | tf_op jit(solution)/shard_map/pallas_call | solution.py:857
  59.6 2.5 %collective-permute-start.6 = (f32[152,128]{1,0:T(8,128)S(1)}, f32[152,128]{1,0:T(8,128)S(1)}, u32[]{:S(2)}, u32[]{:S(2)}) collective-permute-start(f32[152,128]{1,0:T(8,128)S(1)} %get-tuple-element.35.rec0), channel_id=1, source_target_pairs={{0,3},{1,0},{2,1},{3,2},{4,7},{5,4},{6,5},{7,6},{8,11},{9,8},{10,9... | collective-permute-start | bytes 233480 | tf_op jit(solution)/shard_map/ppermute | solution.py:863
  62.0 0.5 collective-permute-start.5
  62.5 0.6 collective-permute-start.4
  63.2 0.3 collective-permute-done.6.rec3
  63.5 3.4 %collective-permute-done.5.rec2 = f32[152,128]{1,0:T(8,128)S(1)} collective-permute-done((f32[152,128]{1,0:T(8,128)S(1)}, f32[152,128]{1,0:T(8,128)S(1)}, u32[]{:S(2)}, u32[]{:S(2)}) %collective-permute-start.5) | collective-permute-done | bytes 77856 | tf_op jit(solution)/shard_map/ppermute | solution.py:863
  66.8 2.1 %collective-permute-done.4.rec1 = f32[152,128]{1,0:T(8,128)S(1)} collective-permute-done((f32[152,128]{1,0:T(8,128)S(1)}, f32[152,128]{1,0:T(8,128)S(1)}, u32[]{:S(2)}, u32[]{:S(2)}) %collective-permute-start.4) | collective-permute-done | bytes 77856 | tf_op jit(solution)/shard_map/ppermute | solution.py:863
  69.0 0.0 copy-done
  69.0 1.4 %shard_map.108 = f32[59,2048]{1,0:T(8,128)} custom-call(f32[59,2048]{1,0:T(8,128)S(1)} %copy-done, f32[152,128]{1,0:T(8,128)S(1)} %get-tuple-element.35.rec0, f32[152,128]{1,0:T(8,128)S(1)} %collective-permute-done.4.rec1, f32[152,128]{1,0:T(8,128)S(1)} %collective-permute-done.5.rec2, f32[152,128]{1,0:T(8,128)S(1)} %collective-permute-done.6.rec3), custom_call_target="tpu_custom_call" | custom-call | tf_op jit(solution)/shard_map/pallas_call | solution.py:866
  (3 shorter events, 0.0 us)
Async XLA Ops:
  3.5 13.3 %copy-start.1 = (f32[1,3,16,512]{3,2,1,0:T(8,128)S(1)}, f32[1,3,16,512]{3,2,1,0:T(8,128)}, u32[]{:S(2)}) copy-start(f32[1,3,16,512]{3,2,1,0:T(8,128)} %own.1) | copy-start | bytes 294916
  3.5 23.9 %all-to-all-start = ((f32[64,1,384]{2,1,0:T(1,128)}), f32[64,1,384]{2,1,0:T(1,128)S(1)}, u32[]{:S(2)}, u32[]{:S(2)}) async-start(f32[64,1,384]{2,1,0:T(1,128)} %shard_map.103), calls=%async_computation | async-start | bytes 196608 | tf_op jit(solution)/shard_map/all_to_all | solution.py:795
  16.8 15.9 %collective-permute-start.3 = (f32[3,10,512]{2,1,0:T(8,128)S(1)}, f32[3,10,512]{2,1,0:T(8,128)S(1)}, u32[]{:S(2)}, u32[]{:S(2)}) collective-permute-start(f32[3,10,512]{2,1,0:T(8,128)S(1)} %get-tuple-element.37), channel_id=1, source_target_pairs={{4,8},{8,4},{12,16},{16,12},{20,24},{24,20},{28,32},{32,28},{36,40... | collective-permute-start | bytes 184328 | tf_op jit(solution)/shard_map/ppermute | solution.py:778
  20.4 12.4 %collective-permute-start.2 = (f32[3,10,512]{2,1,0:T(8,128)S(1)}, f32[3,10,512]{2,1,0:T(8,128)S(1)}, u32[]{:S(2)}, u32[]{:S(2)}) collective-permute-start(f32[3,10,512]{2,1,0:T(8,128)S(1)} %get-tuple-element.38), channel_id=1, source_target_pairs={{0,4},{4,0},{8,12},{12,8},{16,20},{20,16},{24,28},{28,24},{32,36},... | collective-permute-start | bytes 184328 | tf_op jit(solution)/shard_map/ppermute | solution.py:777
  27.3 5.4 %copy-start.3 = (s32[1,128,16]{1,2,0:T(8,128)S(1)}, s32[1,128,16]{1,2,0:T(8,128)}, u32[]{:S(2)}) copy-start(s32[1,128,16]{1,2,0:T(8,128)} %param.9) | copy-start | bytes 24580
  30.1 4.5 %collective-permute-start = (f32[3,10,512]{2,1,0:T(8,128)S(1)}, f32[3,10,512]{2,1,0:T(8,128)S(1)}, u32[]{:S(2)}, u32[]{:S(2)}) collective-permute-start(f32[3,10,512]{2,1,0:T(8,128)S(1)} %get-tuple-element.21), channel_id=1, source_target_pairs={{0,4},{4,0},{8,12},{12,8},{16,20},{20,16},{24,28},{28,24},{32,36},... | collective-permute-start | bytes 184328 | tf_op jit(solution)/shard_map/ppermute | solution.py:823
  30.5 6.1 %copy-start.2 = (f32[1,3,16,512]{3,2,1,0:T(8,128)S(1)}, f32[1,3,16,512]{3,2,1,0:T(8,128)}, u32[]{:S(2)}) copy-start(f32[1,3,16,512]{3,2,1,0:T(8,128)} %get-tuple-element.18.strip_ref) | copy-start | bytes 294916
  30.5 6.1 %collective-permute-start.1 = (f32[3,10,512]{2,1,0:T(8,128)S(1)}, f32[3,10,512]{2,1,0:T(8,128)S(1)}, u32[]{:S(2)}, u32[]{:S(2)}) collective-permute-start(f32[3,10,512]{2,1,0:T(8,128)S(1)} %get-tuple-element.22), channel_id=1, source_target_pairs={{4,8},{8,4},{12,16},{16,12},{20,24},{24,20},{28,32},{32,28},{36,40... | collective-permute-start | bytes 184328 | tf_op jit(solution)/shard_map/ppermute | solution.py:824
  36.5 32.4 %copy-start = (f32[59,2048]{1,0:T(8,128)S(1)}, f32[59,2048]{1,0:T(8,128)}, u32[]{:S(2)}) copy-start(f32[59,2048]{1,0:T(8,128)} %p_ref.1) | copy-start | bytes 1449988
  59.6 3.9 %collective-permute-start.6 = (f32[152,128]{1,0:T(8,128)S(1)}, f32[152,128]{1,0:T(8,128)S(1)}, u32[]{:S(2)}, u32[]{:S(2)}) collective-permute-start(f32[152,128]{1,0:T(8,128)S(1)} %get-tuple-element.35.rec0), channel_id=1, source_target_pairs={{0,3},{1,0},{2,1},{3,2},{4,7},{5,4},{6,5},{7,6},{8,11},{9,8},{10,9... | collective-permute-start | bytes 233480 | tf_op jit(solution)/shard_map/ppermute | solution.py:863
  62.0 4.8 %collective-permute-start.5 = (f32[152,128]{1,0:T(8,128)S(1)}, f32[152,128]{1,0:T(8,128)S(1)}, u32[]{:S(2)}, u32[]{:S(2)}) collective-permute-start(f32[152,128]{1,0:T(8,128)S(1)} %get-tuple-element.35.rec0), channel_id=1, source_target_pairs={{0,2},{1,3},{2,0},{3,1},{4,6},{5,7},{6,4},{7,5},{8,10},{9,11},{10,... | collective-permute-start | bytes 233480 | tf_op jit(solution)/shard_map/ppermute | solution.py:863
  62.5 6.4 %collective-permute-start.4 = (f32[152,128]{1,0:T(8,128)S(1)}, f32[152,128]{1,0:T(8,128)S(1)}, u32[]{:S(2)}, u32[]{:S(2)}) collective-permute-start(f32[152,128]{1,0:T(8,128)S(1)} %get-tuple-element.35.rec0), channel_id=1, source_target_pairs={{0,1},{1,2},{2,3},{3,0},{4,5},{5,6},{6,7},{7,4},{8,9},{9,10},{10,1... | collective-permute-start | bytes 233480 | tf_op jit(solution)/shard_map/ppermute | solution.py:863

commit v2 on v1

--- a/solution.py
+++ b/solution.py
@@ -139,19 +139,23 @@
     return jnp.take_along_axis(natural, order, axis=1), order
 
 
-def to_message(out_ref, table):
+def to_message(out_ref, table, twice=False):
     first = table[0:LANES, :].T
     rest = jnp.concatenate(
         [table[LANES:TABLE, :], jnp.zeros((2 * LANES - TABLE, LANES), F32)], axis=0
     ).T
-    out_ref[:, 0, 0:LANES] = first[0:64]
-    out_ref[:, 0, LANES : 2 * LANES] = first[64:128]
-    out_ref[:, 0, 2 * LANES : 3 * LANES] = rest[0:64] + pltpu.roll(rest[64:128], 64, 1)
-
-
-def from_message(in_ref):
-    first = jnp.concatenate([in_ref[:, 0:LANES], in_ref[:, LANES : 2 * LANES]], axis=0).T
-    both = in_ref[:, 2 * LANES : 3 * LANES]
+    parts = [first[0:64], first[64:128], rest[0:64] + pltpu.roll(rest[64:128], 64, 1)]
+    if twice:
+        even = iota((64, LANES), 0) % 2 == 0
+        parts += [jnp.where(even, pltpu.roll(x, 1, 0), pltpu.roll(x, 63, 0)) for x in parts]
+    for i, part in enumerate(parts):
+        out_ref[:, 0, i * LANES : (i + 1) * LANES] = part
+
+
+def from_message(in_ref, start=0):
+    part = lambda i: in_ref[:, (start + i) * LANES : (start + i + 1) * LANES]
+    first = jnp.concatenate([part(0), part(1)], axis=0).T
+    both = part(2)
     rest = jnp.concatenate([both, pltpu.roll(both, 64, 1)], axis=0)
     return first, rest.T, rest
 
@@ -245,7 +249,7 @@
         jnp.where(iota((1, 64), 1) == me, rank_ref[...], 0).astype(F32), axis=1, keepdims=True
     )
     meta = [ids, jnp.broadcast_to(rank, (1, LANES))] + spread(bg_ref) + angles
-    to_message(out_ref, jnp.concatenate(channels + meta, axis=0))
+    to_message(out_ref, jnp.concatenate(channels + meta, axis=0), twice=True)
 
 
 def across(chunks):
@@ -282,7 +286,7 @@
         ext[j, 40:48, :] = jnp.zeros((8, LANES), F32)
         near, far = chip[ch, :, cols], next_chip[ch, :, cols]
         ext[j, 6:16, :] = jnp.where(even, far, near)
-        ext[j, 16:32, :] = own[0, ch, :, cols]
+        ext[j, 16:32, :] = own[ch, :, cols]
         ext[j, 32:42, :] = jnp.where(even, near, far)
 
 
@@ -290,7 +294,7 @@
     even = lax.axis_index("space") % 2 == 0
 
     def channel(ch, carry):
-        fill_rows(tmp, own, chip, next_chip, ch, even)
+        fill_rows(tmp, own.at[0], chip, next_chip, ch, even)
         for j in range(CHUNKS):
             ext_ref[ch, j] = tmp[j]
             sq[j] = tmp[j] * tmp[j]
@@ -350,30 +354,7 @@
     return x0 - get(0), dy, get(2) * -0.5, get(3) * dy, get(4) * -0.5 * dy * dy, get(5)
 
 
-def blend_kernel(
-    recv_ref,
-    strip_ref,
-    chip_ref,
-    next_ref,
-    rec,
-    colour_ref,
-    before_ref,
-    total_ref,
-    nearer_ref,
-    through_ref,
-    alphas,
-    weights,
-    logs,
-    blocks_ref,
-):
-    me = lax.axis_index("space")
-    first, rest_rows, rest_cols = from_message(recv_ref)
-    rec[0:LANES, :] = first
-    rec[LANES:TABLE, :] = rest_rows[0:24]
-    ids = row(rest_rows, 16, 8)
-    corner_x, corner_y = corners(ids, me)
-    y_grid = corner_y + iota((8, LANES), 0).astype(F32)
-
+def render(rec, corner_x, y_grid, logs, colours_out, keep=None):
     def group(g, carry):
         base = corner_x + (g * GROUP).astype(F32)
 
@@ -383,16 +364,20 @@
             for k4 in range(4):
                 k = kk * 4 + k4
                 dx0, dy, ma, mb_y, mc_yy, opacity = splat_terms(rec, k, base, y_grid)
-                tint = [jnp.broadcast_to(rec[pl.ds((6 + c) * K + k, 1), :], (8, LANES)) for c in range(3)]
+                tint = [
+                    jnp.broadcast_to(rec[pl.ds((6 + c) * K + k, 1), :], (8, LANES))
+                    for c in range(3)
+                ]
                 for i in range(GROUP):
                     dx = dx0 + float(i)
                     alpha = opacity * jnp.exp((ma * dx - mb_y) * dx + mc_yy)
                     weight = alpha * through[i]
-                    alphas[k, g * GROUP + i] = alpha
-                    weights[k, g * GROUP + i] = weight
-                    keep = 1.0 - alpha
-                    through = through[:i] + (through[i] * keep,) + through[i + 1 :]
-                    part[i] = part[i] * keep
+                    if keep:
+                        keep[0][k, g * GROUP + i] = alpha
+                        keep[1][k, g * GROUP + i] = weight
+                    left = 1.0 - alpha
+                    through = through[:i] + (through[i] * left,) + through[i + 1 :]
+                    part[i] = part[i] * left
                     colours = (
                         colours[:i]
                         + (tuple(colours[i][c] + weight * tint[c] for c in range(3)),)
@@ -402,25 +387,21 @@
             return through, log_sum, colours
 
         zero = jnp.zeros((8, LANES), F32)
-        through, log_sum, colours = lax.fori_loop(
-            0,
-            4,
-            four,
-            (
-                (jnp.ones((8, LANES), F32),) * GROUP,
-                (zero,) * GROUP,
-                ((zero,) * 3,) * GROUP,
-            ),
-        )
+        start = ((jnp.ones((8, LANES), F32),) * GROUP, (zero,) * GROUP, ((zero,) * 3,) * GROUP)
+        through, log_sum, colours = lax.fori_loop(0, 4, four, start)
         for i in range(GROUP):
             rows = pl.ds(pl.multiple_of((g * GROUP + i) * 8, 8), 8)
             logs[rows, :] = log_sum[i]
-            through_ref[rows, :] = through[i]
+            if keep:
+                keep[2][rows, :] = through[i]
             for c in range(3):
-                colour_ref[c, rows, :] = colours[i][c]
+                colours_out[c, rows, :] = colours[i][c]
         return carry
 
     lax.fori_loop(0, 16 // GROUP, group, 0)
+
+
+def masks(rest_rows, rest_cols):
     id_row = row(rest_rows, 16, LANES)
     rank_row = row(rest_rows, 17, LANES)
     id_col = jnp.broadcast_to(rest_cols[:, 16:17], (LANES, LANES))
@@ -428,19 +409,17 @@
     live = id_row >= 0.0
     same = jnp.where((id_row == id_col) & live, 1.0, 0.0)
     nearer = jnp.where(rank_col < rank_row, same, 0.0).astype(BF16)
-    member = jnp.where(id_col == (iota((LANES, LANES), 1) % 64).astype(F32), 1.0, 0.0).astype(BF16)
-    nearer_ref[...] = nearer
-    log_all = logs[...]
-    ahead = dot_mask(
-        log_all, jnp.concatenate([nearer, same.astype(BF16), member], axis=1), 0
-    )
-    before = jnp.where(live, jnp.exp(ahead[:, 0:LANES]), 0.0)
-    before_ref[...] = before
-    total_ref[...] = jnp.where(live, jnp.exp(ahead[:, LANES : 2 * LANES]), 0.0)
-    open_sky = jnp.exp(ahead[:, 2 * LANES : 3 * LANES])
+    block = (iota((LANES, LANES), 1) % 64).astype(F32)
+    member = jnp.where(id_col == block, 1.0, 0.0).astype(BF16)
+    return live, same.astype(BF16), nearer, member
+
+
+def to_rows(before, open_sky, colours, member, sky_rows, blocks_ref, strip_ref):
     lane = iota((8, LANES), 1)
     for c in range(3):
-        blocks_ref[c] = dot_mask(before * colour_ref[c], member, 0) + rest_rows[18 + c : 19 + c] * open_sky
+        blocks_ref[c] = (
+            dot_mask(before * colours[c], member, 0) + sky_rows[18 + c : 19 + c] * open_sky
+        )
     pair = lane % 16 // 2
     for c in range(3):
         for p in range(8):
@@ -460,12 +439,61 @@
                     )
                     values[c] = jnp.where(pair == p, got, values[c]) if p else got
             for c in range(3):
-                strip_ref[0, c, br * 8 : br * 8 + 8, t * LANES : (t + 1) * LANES] = values[c]
+                strip_ref[c, br * 8 : br * 8 + 8, t * LANES : (t + 1) * LANES] = values[c]
+
+
+def blend_kernel(
+    recv_ref,
+    strip_ref,
+    chip_ref,
+    far_ref,
+    rec,
+    colour_ref,
+    before_ref,
+    total_ref,
+    nearer_ref,
+    through_ref,
+    alphas,
+    weights,
+    logs,
+    blocks_ref,
+    far_rec,
+    far_colour,
+    far_strip,
+):
+    me = lax.axis_index("space")
     even = me % 2 == 0
-    top = strip_ref[0, :, 0:10, :]
-    bottom = strip_ref[0, :, 6:16, :]
-    chip_ref[...] = jnp.where(even, bottom, top)
-    next_ref[...] = jnp.where(even, top, bottom)
+    row_of = iota((8, LANES), 0).astype(F32)
+
+    first, rest_rows, rest_cols = from_message(recv_ref)
+    rec[0:LANES, :] = first
+    rec[LANES:TABLE, :] = rest_rows[0:24]
+    corner_x, corner_y = corners(row(rest_rows, 16, 8), me)
+    render(rec, corner_x, corner_y + row_of, logs, colour_ref, (alphas, weights, through_ref))
+    live, same, nearer, member = masks(rest_rows, rest_cols)
+    nearer_ref[...] = nearer
+    ahead = dot_mask(logs[...], jnp.concatenate([nearer, same, member], axis=1), 0)
+    before = jnp.where(live, jnp.exp(ahead[:, 0:LANES]), 0.0)
+    before_ref[...] = before
+    total_ref[...] = jnp.where(live, jnp.exp(ahead[:, LANES : 2 * LANES]), 0.0)
+    to_rows(
+        before, jnp.exp(ahead[:, 2 * LANES :]), colour_ref, member, rest_rows, blocks_ref, strip_ref
+    )
+    chip_ref[...] = jnp.where(even, strip_ref[:, 6:16, :], strip_ref[:, 0:10, :])
+
+    first, rest_rows, rest_cols = from_message(recv_ref, 3)
+    far_rec[0:LANES, :] = first
+    far_rec[LANES:TABLE, :] = rest_rows[0:24]
+    corner_x, corner_y = corners(row(rest_rows, 16, 8), jnp.where(even, me - 1, me + 1))
+    render(far_rec, corner_x, corner_y + row_of, logs, far_colour)
+    live, _, nearer, member = masks(rest_rows, rest_cols)
+    ahead = dot_mask(logs[...], jnp.concatenate([nearer, member], axis=1), 0)
+    before = jnp.where(live, jnp.exp(ahead[:, 0:LANES]), 0.0)
+    to_rows(
+        before, jnp.exp(ahead[:, LANES:]), far_colour, member, rest_rows, blocks_ref, far_strip
+    )
+    near_edge = jnp.where(even, far_strip[:, 6:16, :], far_strip[:, 0:10, :])
+    far_ref[...] = jnp.where((me > 0) & (me < 63), near_edge, 0.0)
 
 
 def loss_kernel(
@@ -484,6 +512,7 @@
     alphas,
     weights,
     out_ref,
+    rendered_ref,
     ext,
     prod,
     stat,
@@ -494,7 +523,10 @@
     behind_cot,
     sums,
     table,
+    sems,
 ):
+    copy = pltpu.make_async_copy(strip_ref, rendered_ref, sems.at[0])
+    copy.start()
     me = lax.axis_index("space")
     first_c, second_c = SSIM_FIRST, SSIM_SECOND
     even = me % 2 == 0
@@ -653,6 +685,7 @@
         [jnp.broadcast_to(loss, (5, LANES)), rec[META + 5 : TABLE, :]], axis=0
     )
     to_message(out_ref, table[...])
+    copy.wait()
 
 
 def gather_kernel(recv_ref, inv_ref, out_ref, loss_ref, rec):
@@ -751,13 +784,19 @@
             ]
 
 
-def call(kernel, outs, scratch=(), copied=0):
-    extra = {"in_specs": [pl.BlockSpec(memory_space=pltpu.HBM)] * copied} if copied else {}
-    sems = [pltpu.SemaphoreType.DMA((copied,))] if copied else []
+def call(kernel, outs, scratch=(), copied=0, leaving=0):
+    hbm, vmem = (pl.BlockSpec(memory_space=space) for space in (pltpu.HBM, pltpu.VMEM))
+    extra = {}
+    if copied:
+        extra["in_specs"] = [hbm] * copied
+    if leaving:
+        extra["out_specs"] = [vmem] * (len(outs) - leaving) + [hbm] * leaving
+    count = copied + leaving
     return pl.pallas_call(
         kernel,
         out_shape=[jax.ShapeDtypeStruct(shape, dtype) for shape, dtype in outs],
-        scratch_shapes=[pltpu.VMEM(shape, dtype) for shape, dtype in scratch] + sems,
+        scratch_shapes=[pltpu.VMEM(shape, dtype) for shape, dtype in scratch]
+        + ([pltpu.SemaphoreType.DMA((count,))] if count else []),
         compiler_params=pltpu.CompilerParams(vmem_limit_bytes=(60 if copied else 16) << 20),
         **extra,
     )
@@ -778,7 +817,7 @@
     goal_next = lax.ppermute(jnp.where(even, goal_top, goal_bottom), "space", next_chip)
     (message,) = call(
         send_kernel,
-        [((64, 1, 384), F32)],
+        [((64, 1, 768), F32)],
         [
             (params.shape, F32),
             ((1, 3), F32),
@@ -792,7 +831,7 @@
         ],
         copied=7,
     )(params, camera, lists, blocks, counts, depth_rank, background)
-    received = lax.all_to_all(message, "space", 0, 0, tiled=True).reshape(64, 384)
+    received = lax.all_to_all(message, "space", 0, 0, tiled=True).reshape(64, 768)
     goal, goal_mean, goal_square, inverse = call(
         target_kernel,
         [
@@ -803,10 +842,10 @@
         ],
         [((CHUNKS, 48, LANES), F32)] * 2,
     )(target, goal_chip, goal_next, lists)
-    strip, to_chip, to_next, records, colours, before, total, nearer, through, alphas, weights = call(
+    strip, to_chip, far, records, colours, before, total, nearer, through, alphas, weights = call(
         blend_kernel,
         [
-            ((1, 3, 16, 512), F32),
+            ((3, 16, 512), F32),
             ((3, 10, 512), F32),
             ((3, 10, 512), F32),
             ((TABLE, LANES), F32),
@@ -818,13 +857,18 @@
             kept,
             kept,
         ],
-        [(tile, F32), ((3, *tile), F32)],
+        [
+            (tile, F32),
+            ((3, *tile), F32),
+            ((TABLE, LANES), F32),
+            ((3, *tile), F32),
+            ((3, 16, 512), F32),
+        ],
     )(received)
     strip_chip = lax.ppermute(to_chip, "space", chip)
-    strip_next = lax.ppermute(to_next, "space", next_chip)
-    (reply,) = call(
+    reply, rendered = call(
         loss_kernel,
-        [((64, 1, 384), F32)],
+        [((64, 1, 384), F32), ((3, 16, 512), F32)],
         [
             ((CHUNKS, 48, LANES), F32),
             ((2, CHUNKS, 48, LANES), F32),
@@ -837,10 +881,11 @@
             ((K, 6, 8, LANES), F32),
             ((TABLE, LANES), F32),
         ],
+        leaving=1,
     )(
         strip,
         strip_chip,
-        strip_next,
+        far,
         goal,
         goal_mean,
         goal_square,
@@ -868,7 +913,7 @@
         [((59, 2048), F32)],
         [((8, LANES, LANES), F32), ((4, TABLE, LANES), F32), ((8, LANES, LANES), F32)],
     )(params, record_grads, *others)
-    return (grad_params, strip, loss[0, 0:1])
+    return (grad_params, rendered[None], loss[0, 0:1])
 
 
 def solution(mesh):

time: 70.7 us -> 66.4 us (0.939)
  blocking collectives: 17.3 us -> 14.7 us
  starting transfers between devices: 23.2 us -> 21 us
  Pallas kernels: 14.4 us -> 15.5 us
    all_to_all x1, blocking collectives: 17.3 us -> 14.7 us  [shards(): returned = lax.all_to_all(reply, 'space', 0, 0, tiled=True).reshape(64, 384)]
    ppermute x1 -> x0, starting transfers between devices: 2.24 us -> none  [shards(): strip_next = lax.ppermute(to_next, 'space', next_chip)]
    ppermute x1 -> x0, waiting for transfers between devices: 1.98 us -> none  [shards(): strip_next = lax.ppermute(to_next, 'space', next_chip)]
    all_to_all x1, waiting for transfers between devices: 6.86 us -> 8.33 us  [shards(): lax.all_to_all(message, 'space', 0, 0, tiled=True).reshape(64, 768)]
    pallas_call x3, Pallas kernels: 10.3 us -> 11.3 us  [the longest x1 4.75 us: shards(): call(loss_kernel, [((64, 1, 384), F32), ((3, 16, 512), F32)], [((CHUNKS,...]
  transfers between devices with their start and end apart: 8 -> 7, of which waited for: 5 -> 4; matrix products, arithmetic and copies ran while one was open for 0% -> 0% of each run, Pallas kernels for 6% -> 9%
where the time goes in v2:
time: 66.4 us; the launch traced here: 66.2 us
  starting transfers between devices  21 us (32%)
  Pallas kernels  15.5 us (23%)
  blocking collectives  14.7 us (22%)
  waiting for transfers between devices  14.1 us (21%)
  between operations  0.76 us (1%)
    all_to_all x1, blocking collectives, shards(): returned = lax.all_to_all(reply, 'space', 0, 0, tiled=True).reshape(64, 384)  14.7 us
    all_to_all x1, starting transfers between devices, shards(): lax.all_to_all(message, 'space', 0, 0, tiled=True).reshape(64, 768)  13.3 us
    all_to_all x1, waiting for transfers between devices, shards(): lax.all_to_all(message, 'space', 0, 0, tiled=True).reshape(64, 768)  8.33 us
    ppermute x3, waiting for transfers between devices, shards(): lax.ppermute(record_grads, 'view', [(i, (i + d) % views) for i in range(v...  5.79 us
    pallas_call x1, Pallas kernels, shards(): call(loss_kernel, [((64, 1, 384), F32), ((3, 16, 512), F32)], [((CHUNKS,...  4.75 us
    pallas_call x1, Pallas kernels, shards(): call(blend_kernel, [((3, 16, 512), F32), ((3, 10, 512), F32), ((3, 10, 51...  3.91 us
    ppermute x3, starting transfers between devices, shards(): lax.ppermute(record_grads, 'view', [(i, (i + d) % views) for i in range(v...  3.61 us
    ppermute x1, starting transfers between devices, shards(): lax.ppermute(jnp.where(even, goal_top, goal_bottom), 'space', next_chip)  3.54 us
  transfers between devices with their start and end apart: 7, of which 4 were waited for; matrix products, arithmetic and copies ran while one was open for 0% of the time, Pallas kernels for 9%

profile of v2, /device:TPU:1, one launch (start us, length us, event | category | flops | bytes accessed | tf_op | source)
XLA Modules:
  0.0 66.2 jit_solution(3981478802252554692)
XLA Ops:
  0.6 2.7 %shard_map.103 = f32[64,1,768]{2,1,0:T(1,128)} custom-call(f32[59,2048]{1,0:T(8,128)} %p_ref.1, f32[1,3]{1,0:T(1,128)} %cam_hbm.1, s32[16,128]{1,0:T(8,128)} %bitcast.18, s32[1,128]{1,0:T(1,128)} %blk_hbm.1, s32[1,64]{1,0:T(1,128)} %cnt_hbm.1, s32[1,64]{1,0:T(1,128)} %rank_hbm.1, f32[1,3]{1,0:T(1,128)} %bg_hbm.1), custom_call_target="tpu_custom_call" | custom-call | tf_op jit(solution)/shard_map/pallas_call | solution.py:818
  3.3 0.0 copy-start.1
  3.3 13.3 %all-to-all-start = ((f32[64,1,768]{2,1,0:T(1,128)}), f32[64,1,768]{2,1,0:T(1,128)S(1)}, u32[]{:S(2)}, u32[]{:S(2)}) async-start(f32[64,1,768]{2,1,0:T(1,128)} %shard_map.103), calls=%async_computation | async-start | bytes 393216 | tf_op jit(solution)/shard_map/all_to_all | solution.py:834
  16.6 0.0 copy-done.1
  16.7 3.5 %collective-permute-start.2 = (f32[3,10,512]{2,1,0:T(8,128)S(1)}, f32[3,10,512]{2,1,0:T(8,128)S(1)}, u32[]{:S(2)}, u32[]{:S(2)}) collective-permute-start(f32[3,10,512]{2,1,0:T(8,128)S(1)} %get-tuple-element.41), channel_id=1, source_target_pairs={{4,8},{8,4},{12,16},{16,12},{20,24},{24,20},{28,32},{32,28},{36,40... | collective-permute-start | bytes 184328 | tf_op jit(solution)/shard_map/ppermute | solution.py:817
  20.2 0.1 collective-permute-start.1
  20.3 8.3 %all-to-all-done = f32[64,1,768]{2,1,0:T(1,128)S(1)} async-done(((f32[64,1,768]{2,1,0:T(1,128)}), f32[64,1,768]{2,1,0:T(1,128)S(1)}, u32[]{:S(2)}, u32[]{:S(2)}) %all-to-all-start) | async-done | bytes 196640 | tf_op jit(solution)/shard_map/all_to_all | solution.py:834
  28.7 0.0 copy-start.2
  28.7 3.9 %shard_map.104 = (f32[3,16,512]{2,1,0:T(8,128)S(1)}, f32[3,10,512]{2,1,0:T(8,128)S(1)}, f32[3,10,512]{2,1,0:T(8,128)S(1)}, f32[152,128]{1,0:T(8,128)S(1)}, f32[3...) custom-call(f32[64,768]{1,0:T(8,128)S(1)} %bitcast.16), custom_call_target="tpu_custom_call" | custom-call | tf_op jit(solution)/shard_map/pallas_call | solution.py:845
  32.6 0.5 collective-permute-start
  33.1 0.0 collective-permute-done.2.next_chip
  33.1 0.0 collective-permute-done.1.chip
  33.1 0.0 copy-done.2
  33.1 1.8 %shard_map.105 = (f32[3,4,48,128]{3,2,1,0:T(8,128)S(1)}, f32[3,4,32,128]{3,2,1,0:T(8,128)S(1)}, f32[3,4,32,128]{3,2,1,0:T(8,128)S(1)}, s32[32,128]{1,0:T(8,128)S(1)}) custom-call(f32[1,3,16,512]{3,2,1,0:T(8,128)S(1)} %copy-done.1, f32[3,10,512]{2,1,0:T(8,128)S(1)} %collective-permute-done.1.chip, f32[3,10,512]{2,1,0:T(8,128)S(1)} %collective-permute-done.2.next_chip, ...), custom_call_target="tpu_custom_call" | custom-call | tf_op jit(solution)/shard_map/pallas_call | solution.py:835
  34.8 0.0 collective-permute-done.chip
  34.9 0.0 copy-start
  34.9 4.8 %shard_map.106 = (f32[64,1,384]{2,1,0:T(1,128)S(1)}, f32[3,16,512]{2,1,0:T(8,128)}) custom-call(f32[3,16,512]{2,1,0:T(8,128)S(1)} %get-tuple-element.22.strip_ref, f32[3,10,512]{2,1,0:T(8,128)S(1)} %collective-permute-done.chip, f32[3,10,512]{2,1,0:T(8,128)S(1)} %get-tuple-element.24.next_chip, f32[3,4,48,128]{3,2,1,0:T(8,128)S(1)} %get-tuple-element.25.ext_ref, ...), custom_call_target="tpu_custom_call" | custom-call | tf_op jit(solution)/shard_map/pallas_call | solution.py:869
  39.6 14.7 %all_to_all.10 = f32[64,1,384]{2,1,0:T(1,128)S(1)} all-to-all(f32[64,1,384]{2,1,0:T(1,128)S(1)} %get-tuple-element.36), channel_id=1, replica_groups=mesh['space'=64,'view'=4] {'space'}, dimensions={0} | all-to-all | bytes 196608 | tf_op jit(solution)/shard_map/all_to_all | solution.py:901
  54.4 1.0 %shard_map.107 = (f32[152,128]{1,0:T(8,128)S(1)}, f32[1,128]{1,0:T(1,128)}) custom-call(f32[64,384]{1,0:T(8,128)S(1)} %bitcast.17, s32[32,128]{1,0:T(8,128)S(1)} %get-tuple-element.37.inv_ref), custom_call_target="tpu_custom_call" | custom-call | tf_op jit(solution)/shard_map/pallas_call | solution.py:902
  55.4 2.5 %collective-permute-start.5 = (f32[152,128]{1,0:T(8,128)S(1)}, f32[152,128]{1,0:T(8,128)S(1)}, u32[]{:S(2)}, u32[]{:S(2)}) collective-permute-start(f32[152,128]{1,0:T(8,128)S(1)} %get-tuple-element.38.rec0), channel_id=1, source_target_pairs={{0,3},{1,0},{2,1},{3,2},{4,7},{5,4},{6,5},{7,6},{8,11},{9,8},{10,9... | collective-permute-start | bytes 233480 | tf_op jit(solution)/shard_map/ppermute | solution.py:908
  57.9 0.5 collective-permute-start.4
  58.4 0.6 collective-permute-start.3
  59.0 0.3 collective-permute-done.5.rec3
  59.3 3.4 %collective-permute-done.4.rec2 = f32[152,128]{1,0:T(8,128)S(1)} collective-permute-done((f32[152,128]{1,0:T(8,128)S(1)}, f32[152,128]{1,0:T(8,128)S(1)}, u32[]{:S(2)}, u32[]{:S(2)}) %collective-permute-start.4) | collective-permute-done | bytes 77856 | tf_op jit(solution)/shard_map/ppermute | solution.py:908
  62.7 2.1 %collective-permute-done.3.rec1 = f32[152,128]{1,0:T(8,128)S(1)} collective-permute-done((f32[152,128]{1,0:T(8,128)S(1)}, f32[152,128]{1,0:T(8,128)S(1)}, u32[]{:S(2)}, u32[]{:S(2)}) %collective-permute-start.3) | collective-permute-done | bytes 77856 | tf_op jit(solution)/shard_map/ppermute | solution.py:908
  64.8 0.0 copy-done
  64.8 1.4 %shard_map.108 = f32[59,2048]{1,0:T(8,128)} custom-call(f32[59,2048]{1,0:T(8,128)S(1)} %copy-done, f32[152,128]{1,0:T(8,128)S(1)} %get-tuple-element.38.rec0, f32[152,128]{1,0:T(8,128)S(1)} %collective-permute-done.3.rec1, f32[152,128]{1,0:T(8,128)S(1)} %collective-permute-done.4.rec2, f32[152,128]{1,0:T(8,128)S(1)} %collective-permute-done.5.rec3), custom_call_target="tpu_custom_call" | custom-call | tf_op jit(solution)/shard_map/pallas_call | solution.py:911
  (3 shorter events, 0.0 us)
Async XLA Ops:
  3.3 13.3 %copy-start.1 = (f32[1,3,16,512]{3,2,1,0:T(8,128)S(1)}, f32[1,3,16,512]{3,2,1,0:T(8,128)}, u32[]{:S(2)}) copy-start(f32[1,3,16,512]{3,2,1,0:T(8,128)} %own.1) | copy-start | bytes 294916
  3.3 25.3 %all-to-all-start = ((f32[64,1,768]{2,1,0:T(1,128)}), f32[64,1,768]{2,1,0:T(1,128)S(1)}, u32[]{:S(2)}, u32[]{:S(2)}) async-start(f32[64,1,768]{2,1,0:T(1,128)} %shard_map.103), calls=%async_computation | async-start | bytes 393216 | tf_op jit(solution)/shard_map/all_to_all | solution.py:834
  16.7 16.4 %collective-permute-start.2 = (f32[3,10,512]{2,1,0:T(8,128)S(1)}, f32[3,10,512]{2,1,0:T(8,128)S(1)}, u32[]{:S(2)}, u32[]{:S(2)}) collective-permute-start(f32[3,10,512]{2,1,0:T(8,128)S(1)} %get-tuple-element.41), channel_id=1, source_target_pairs={{4,8},{8,4},{12,16},{16,12},{20,24},{24,20},{28,32},{32,28},{36,40... | collective-permute-start | bytes 184328 | tf_op jit(solution)/shard_map/ppermute | solution.py:817
  20.2 12.8 %collective-permute-start.1 = (f32[3,10,512]{2,1,0:T(8,128)S(1)}, f32[3,10,512]{2,1,0:T(8,128)S(1)}, u32[]{:S(2)}, u32[]{:S(2)}) collective-permute-start(f32[3,10,512]{2,1,0:T(8,128)S(1)} %get-tuple-element.42), channel_id=1, source_target_pairs={{0,4},{4,0},{8,12},{12,8},{16,20},{20,16},{24,28},{28,24},{32,36},... | collective-permute-start | bytes 184328 | tf_op jit(solution)/shard_map/ppermute | solution.py:816
  28.7 4.4 %copy-start.2 = (s32[1,128,16]{1,2,0:T(8,128)S(1)}, s32[1,128,16]{1,2,0:T(8,128)}, u32[]{:S(2)}) copy-start(s32[1,128,16]{1,2,0:T(8,128)} %param.9) | copy-start | bytes 24580
  32.6 2.3 %collective-permute-start = (f32[3,10,512]{2,1,0:T(8,128)S(1)}, f32[3,10,512]{2,1,0:T(8,128)S(1)}, u32[]{:S(2)}, u32[]{:S(2)}) collective-permute-start(f32[3,10,512]{2,1,0:T(8,128)S(1)} %get-tuple-element.23), channel_id=1, source_target_pairs={{0,4},{4,0},{8,12},{12,8},{16,20},{20,16},{24,28},{28,24},{32,36},... | collective-permute-start | bytes 184328 | tf_op jit(solution)/shard_map/ppermute | solution.py:868
  34.9 29.9 %copy-start = (f32[59,2048]{1,0:T(8,128)S(1)}, f32[59,2048]{1,0:T(8,128)}, u32[]{:S(2)}) copy-start(f32[59,2048]{1,0:T(8,128)} %p_ref.1) | copy-start | bytes 1449988
  55.4 3.9 %collective-permute-start.5 = (f32[152,128]{1,0:T(8,128)S(1)}, f32[152,128]{1,0:T(8,128)S(1)}, u32[]{:S(2)}, u32[]{:S(2)}) collective-permute-start(f32[152,128]{1,0:T(8,128)S(1)} %get-tuple-element.38.rec0), channel_id=1, source_target_pairs={{0,3},{1,0},{2,1},{3,2},{4,7},{5,4},{6,5},{7,6},{8,11},{9,8},{10,9... | collective-permute-start | bytes 233480 | tf_op jit(solution)/shard_map/ppermute | solution.py:908
  57.9 4.8 %collective-permute-start.4 = (f32[152,128]{1,0:T(8,128)S(1)}, f32[152,128]{1,0:T(8,128)S(1)}, u32[]{:S(2)}, u32[]{:S(2)}) collective-permute-start(f32[152,128]{1,0:T(8,128)S(1)} %get-tuple-element.38.rec0), channel_id=1, source_target_pairs={{0,2},{1,3},{2,0},{3,1},{4,6},{5,7},{6,4},{7,5},{8,10},{9,11},{10,... | collective-permute-start | bytes 233480 | tf_op jit(solution)/shard_map/ppermute | solution.py:908
  58.4 6.4 %collective-permute-start.3 = (f32[152,128]{1,0:T(8,128)S(1)}, f32[152,128]{1,0:T(8,128)S(1)}, u32[]{:S(2)}, u32[]{:S(2)}) collective-permute-start(f32[152,128]{1,0:T(8,128)S(1)} %get-tuple-element.38.rec0), channel_id=1, source_target_pairs={{0,1},{1,2},{2,3},{3,0},{4,5},{5,6},{6,7},{7,4},{8,9},{9,10},{10,1... | collective-permute-start | bytes 233480 | tf_op jit(solution)/shard_map/ppermute | solution.py:908

commit v3 on v2

--- a/solution.py
+++ b/solution.py
@@ -100,8 +100,8 @@
     return [[cell(value) for value in line] for line in turn], [cell(value) for value in basis]
 
 
-def load_params(p_ref, scratch):
-    for tile in range(8):
+def load_params(p_ref, scratch, tiles=8):
+    for tile in range(tiles):
         count = min(8, 59 - tile * 8)
         for chunk in range(16):
             scratch[tile, chunk * 8 : chunk * 8 + count, :] = p_ref[
@@ -144,18 +144,19 @@
     rest = jnp.concatenate(
         [table[LANES:TABLE, :], jnp.zeros((2 * LANES - TABLE, LANES), F32)], axis=0
     ).T
-    parts = [first[0:64], first[64:128], rest[0:64] + pltpu.roll(rest[64:128], 64, 1)]
+    parts = [rest[0:64] + pltpu.roll(rest[64:128], 64, 1), first[0:64], first[64:128]]
     if twice:
         even = iota((64, LANES), 0) % 2 == 0
-        parts += [jnp.where(even, pltpu.roll(x, 1, 0), pltpu.roll(x, 63, 0)) for x in parts]
+        far = [jnp.where(even, pltpu.roll(x, 1, 0), pltpu.roll(x, 63, 0)) for x in parts]
+        parts = [parts[0] + pltpu.roll(far[0], 32, 1)] + parts[1:] + far[1:]
     for i, part in enumerate(parts):
         out_ref[:, 0, i * LANES : (i + 1) * LANES] = part
 
 
-def from_message(in_ref, start=0):
-    part = lambda i: in_ref[:, (start + i) * LANES : (start + i + 1) * LANES]
-    first = jnp.concatenate([part(0), part(1)], axis=0).T
-    both = part(2)
+def from_message(in_ref, far=False):
+    part = lambda i: in_ref[:, i * LANES : (i + 1) * LANES]
+    first = jnp.concatenate([part(3), part(4)] if far else [part(1), part(2)], axis=0).T
+    both = pltpu.roll(part(0), LANES - 32, 1) if far else part(0)
     rest = jnp.concatenate([both, pltpu.roll(both, 64, 1)], axis=0)
     return first, rest.T, rest
 
@@ -290,7 +291,7 @@
         ext[j, 32:42, :] = jnp.where(even, near, far)
 
 
-def target_kernel(own, chip, next_chip, vis_ref, ext_ref, mean_ref, square_ref, inv_ref, tmp, sq):
+def target_kernel(own, chip, next_chip, ext_ref, mean_ref, square_ref, tmp, sq):
     even = lax.axis_index("space") % 2 == 0
 
     def channel(ch, carry):
@@ -305,7 +306,11 @@
                     out[ch, j, top : top + 8, :] = blurred[j]
         return carry
 
-    lax.fori_loop(0, 3, channel, 0)
+    for ch in range(3):
+        channel(ch, 0)
+
+
+def inverse_kernel(vis_ref, inv_ref):
     lists, _ = slot_lists(vis_ref)
     low = lists & 127
     high = lists // LANES
@@ -388,7 +393,7 @@
 
         zero = jnp.zeros((8, LANES), F32)
         start = ((jnp.ones((8, LANES), F32),) * GROUP, (zero,) * GROUP, ((zero,) * 3,) * GROUP)
-        through, log_sum, colours = lax.fori_loop(0, 4, four, start)
+        through, log_sum, colours = lax.fori_loop(0, 4, four, start, unroll=4)
         for i in range(GROUP):
             rows = pl.ds(pl.multiple_of((g * GROUP + i) * 8, 8), 8)
             logs[rows, :] = log_sum[i]
@@ -444,6 +449,7 @@
 
 def blend_kernel(
     recv_ref,
+    order_ref,
     strip_ref,
     chip_ref,
     far_ref,
@@ -481,7 +487,7 @@
     )
     chip_ref[...] = jnp.where(even, strip_ref[:, 6:16, :], strip_ref[:, 0:10, :])
 
-    first, rest_rows, rest_cols = from_message(recv_ref, 3)
+    first, rest_rows, rest_cols = from_message(recv_ref, far=True)
     far_rec[0:LANES, :] = first
     far_rec[LANES:TABLE, :] = rest_rows[0:24]
     corner_x, corner_y = corners(row(rest_rows, 16, 8), jnp.where(even, me - 1, me + 1))
@@ -654,7 +660,7 @@
                 sums[k, n] = jnp.where(g == 0, value, sums[k, n] + value)
             return tuple(after)
 
-        lax.fori_loop(0, K, back, suffix)
+        lax.fori_loop(0, K, back, suffix, unroll=2)
         return carry
 
     lax.fori_loop(0, 16 // GROUP, group, 0)
@@ -680,7 +686,7 @@
             table[pl.ds(ch * K + k, 1), :] = out[ch]
         return carry
 
-    lax.fori_loop(0, K, finish, 0)
+    lax.fori_loop(0, K, finish, 0, unroll=4)
     table[META:TABLE, :] = jnp.concatenate(
         [jnp.broadcast_to(loss, (5, LANES)), rec[META + 5 : TABLE, :]], axis=0
     )
@@ -705,26 +711,50 @@
     loss_ref[...] = jnp.broadcast_to(total * (1.0 / 1572864.0), (1, LANES))
 
 
-def pull_kernel(p_ref, rec0, rec1, rec2, rec3, out_ref, par, views, res):
+def lay_out(rows, start, scratch, out_ref):
+    for n, value in enumerate(rows):
+        index = start + n
+        scratch[index // 8, pl.ds(index % 8, 16, stride=8), :] = value
+    for first in range(start, start + len(rows), 8):
+        count = min(8, start + len(rows) - first)
+        for chunk in range(16):
+            out_ref[first : first + count, chunk * LANES : (chunk + 1) * LANES] = scratch[
+                first // 8, chunk * 8 : chunk * 8 + count, :
+            ]
+
+
+def pull_kernel(p_ref, rec0, rec1, rec2, rec3, out_hbm, par, views, res, out_ref, sems):
     me = lax.axis_index("view")
-    load_params(p_ref, par)
+    load_params(p_ref, par, 2)
     for d, source in enumerate((rec0, rec1, rec2, rec3)):
         views[(me - d + 4) % 4] = source[...]
     get = lambda index: dense_row(par, index)
     scales = [jnp.exp(get(3 + i)) for i in range(3)]
     quaternion, inverse_norm = unit([get(6 + i) for i in range(4)])
     spin = spin_of(quaternion)
+    coefficients = []
+    angles = [
+        [views[v, META + 5 + i : META + 6 + i, :] for i in range(3)] for v in range(4)
+    ]
+    cameras = [camera_values(angles[v]) for v in range(4)]
+    for k in range(16):
+        for c in range(3):
+            rows = slice(96 + 16 * c, 112 + 16 * c)
+            total = cameras[0][1][k] * views[0, rows, :]
+            for v in range(1, 4):
+                total = total + cameras[v][1][k] * views[v, rows, :]
+            coefficients.append(total)
+    lay_out(coefficients[5:], 16, res, out_ref)
+    body = pltpu.make_async_copy(out_ref.at[16:59], out_hbm.at[16:59], sems.at[0])
+    body.start()
     zero = jnp.zeros((16, LANES), F32)
     g_pos = [zero] * 3
     g_frame_spin = [[zero] * 3 for _ in range(3)]
     g_log = [zero] * 3
     g_logit = zero
-    g_colour = []
-    bases = []
     for v in range(4):
-        turn, basis = camera_values([views[v, META + 5 + i : META + 6 + i, :] for i in range(3)])
-        bases.append(basis)
-        g = [views[v, ch * 16 : ch * 16 + 16, :] for ch in range(9)]
+        turn = cameras[v][0]
+        g = [views[v, ch * 16 : ch * 16 + 16, :] for ch in range(6)]
         unscaled = [
             [turn[r][0] * spin[0][c] + turn[r][1] * spin[1][c] + turn[r][2] * spin[2][c] for c in range(3)]
             for r in range(2)
@@ -752,7 +782,6 @@
         for m in range(3):
             g_pos[m] = g_pos[m] + turn[0][m] * g[0] + turn[1][m] * g[1]
         g_logit = g_logit + g[5]
-        g_colour.append(g[6:9])
     s = [[g_frame_spin[m][c] * scales[c] for c in range(3)] for m in range(3)]
     w, x, y, z = quaternion
     g_unit = [
@@ -768,30 +797,21 @@
     g_quat = [(g - q * along) * inverse_norm for q, g in zip(quaternion, g_unit)]
     rest = sigmoid(-get(10))
     rows = g_pos + g_log + g_quat + [g_logit * rest]
-    for k in range(16):
-        for c in range(3):
-            total = bases[0][k] * g_colour[0][c]
-            for v in range(1, 4):
-                total = total + bases[v][k] * g_colour[v][c]
-            rows.append(total)
-    for index in range(59):
-        res[index // 8, pl.ds(index % 8, 16, stride=8), :] = rows[index]
-    for tile in range(8):
-        count = min(8, 59 - tile * 8)
-        for chunk in range(16):
-            out_ref[tile * 8 : tile * 8 + count, chunk * LANES : (chunk + 1) * LANES] = res[
-                tile, chunk * 8 : chunk * 8 + count, :
-            ]
-
-
-def call(kernel, outs, scratch=(), copied=0, leaving=0):
+    lay_out(rows + coefficients[:5], 0, res, out_ref)
+    head = pltpu.make_async_copy(out_ref.at[0:16], out_hbm.at[0:16], sems.at[1])
+    head.start()
+    body.wait()
+    head.wait()
+
+
+def call(kernel, outs, scratch=(), copied=0, leaving=0, sems=0):
     hbm, vmem = (pl.BlockSpec(memory_space=space) for space in (pltpu.HBM, pltpu.VMEM))
     extra = {}
     if copied:
         extra["in_specs"] = [hbm] * copied
     if leaving:
         extra["out_specs"] = [vmem] * (len(outs) - leaving) + [hbm] * leaving
-    count = copied + leaving
+    count = sems or copied + leaving
     return pl.pallas_call(
         kernel,
         out_shape=[jax.ShapeDtypeStruct(shape, dtype) for shape, dtype in outs],
@@ -817,7 +837,7 @@
     goal_next = lax.ppermute(jnp.where(even, goal_top, goal_bottom), "space", next_chip)
     (message,) = call(
         send_kernel,
-        [((64, 1, 768), F32)],
+        [((64, 1, 640), F32)],
         [
             (params.shape, F32),
             ((1, 3), F32),
@@ -831,17 +851,17 @@
         ],
         copied=7,
     )(params, camera, lists, blocks, counts, depth_rank, background)
-    received = lax.all_to_all(message, "space", 0, 0, tiled=True).reshape(64, 768)
-    goal, goal_mean, goal_square, inverse = call(
+    received = lax.all_to_all(message, "space", 0, 0, tiled=True).reshape(64, 640)
+    (inverse,) = call(inverse_kernel, [((32, LANES), I32)])(lists)
+    goal, goal_mean, goal_square = call(
         target_kernel,
         [
             ((3, CHUNKS, 48, LANES), F32),
             ((3, CHUNKS, 32, LANES), F32),
             ((3, CHUNKS, 32, LANES), F32),
-            ((32, LANES), I32),
         ],
         [((CHUNKS, 48, LANES), F32)] * 2,
-    )(target, goal_chip, goal_next, lists)
+    )(target, goal_chip, goal_next)
     strip, to_chip, far, records, colours, before, total, nearer, through, alphas, weights = call(
         blend_kernel,
         [
@@ -864,7 +884,7 @@
             ((3, *tile), F32),
             ((3, 16, 512), F32),
         ],
-    )(received)
+    )(received, inverse)
     strip_chip = lax.ppermute(to_chip, "space", chip)
     reply, rendered = call(
         loss_kernel,
@@ -911,7 +931,14 @@
     (grad_params,) = call(
         pull_kernel,
         [((59, 2048), F32)],
-        [((8, LANES, LANES), F32), ((4, TABLE, LANES), F32), ((8, LANES, LANES), F32)],
+        [
+            ((8, LANES, LANES), F32),
+            ((4, TABLE, LANES), F32),
+            ((8, LANES, LANES), F32),
+            (params.shape, F32),
+        ],
+        leaving=1,
+        sems=2,
     )(params, record_grads, *others)
     return (grad_params, rendered[None], loss[0, 0:1])
 

time: 66.4 us -> 64.4 us (0.970)
  Pallas kernels: 15.5 us -> 14.7 us
  waiting for transfers between devices: 14.1 us -> 13.3 us
    all_to_all x1, waiting for transfers between devices: 8.33 us -> 7.52 us  [shards(): lax.all_to_all(message, 'space', 0, 0, tiled=True).reshape(64, 640)]
    pallas_call x1 -> x2, Pallas kernels: 2.67 us -> 3.2 us  [the longest x1 2.74 us: shards(): call(send_kernel, [((64, 1, 640), F32)], [(params.shape, F32), ((1, 3), F...]
  transfers between devices with their start and end apart: 7 -> 7, of which waited for: 4 -> 4; matrix products, arithmetic and copies ran while one was open for 0% -> 0% of each run, Pallas kernels for 9% -> 8%
where the time goes in v3:
time: 64.4 us; the launch traced here: 64.2 us
  starting transfers between devices  21 us (33%)
  Pallas kernels  14.7 us (23%)
  blocking collectives  14.3 us (22%)
  waiting for transfers between devices  13.3 us (21%)
  between operations  0.77 us (1%)
    all_to_all x1, blocking collectives, shards(): returned = lax.all_to_all(reply, 'space', 0, 0, tiled=True).reshape(64, 384)  14.3 us
    all_to_all x1, starting transfers between devices, shards(): lax.all_to_all(message, 'space', 0, 0, tiled=True).reshape(64, 640)  13.3 us
    all_to_all x1, waiting for transfers between devices, shards(): lax.all_to_all(message, 'space', 0, 0, tiled=True).reshape(64, 640)  7.52 us
    ppermute x3, waiting for transfers between devices, shards(): lax.ppermute(record_grads, 'view', [(i, (i + d) % views) for i in range(v...  5.8 us
    pallas_call x1, Pallas kernels, shards(): call(loss_kernel, [((64, 1, 384), F32), ((3, 16, 512), F32)], [((CHUNKS,...  4.46 us
    ppermute x3, starting transfers between devices, shards(): lax.ppermute(record_grads, 'view', [(i, (i + d) % views) for i in range(v...  3.6 us
    ppermute x1, starting transfers between devices, shards(): lax.ppermute(jnp.where(even, goal_top, goal_bottom), 'space', next_chip)  3.54 us
    pallas_call x1, Pallas kernels, shards(): call(blend_kernel, [((3, 16, 512), F32), ((3, 10, 512), F32), ((3, 10, 51...  3.52 us
  transfers between devices with their start and end apart: 7, of which 4 were waited for; matrix products, arithmetic and copies ran while one was open for 0% of the time, Pallas kernels for 8%

profile of v3, /device:TPU:1, one launch (start us, length us, event | category | flops | bytes accessed | tf_op | source)
XLA Modules:
  0.0 64.2 jit_solution(15813274688860282041)
XLA Ops:
  0.6 2.7 %shard_map.103 = f32[64,1,640]{2,1,0:T(1,128)} custom-call(f32[59,2048]{1,0:T(8,128)} %p_ref.1, f32[1,3]{1,0:T(1,128)} %cam_hbm.1, s32[16,128]{1,0:T(8,128)} %bitcast.18, s32[1,128]{1,0:T(1,128)} %blk_hbm.1, s32[1,64]{1,0:T(1,128)} %cnt_hbm.1, s32[1,64]{1,0:T(1,128)} %rank_hbm.1, f32[1,3]{1,0:T(1,128)} %bg_hbm.1), custom_call_target="tpu_custom_call" | custom-call | tf_op jit(solution)/shard_map/pallas_call | solution.py:838
  3.4 0.0 copy-start.1
  3.4 13.3 %all-to-all-start = ((f32[64,1,640]{2,1,0:T(1,128)}), f32[64,1,640]{2,1,0:T(1,128)S(1)}, u32[]{:S(2)}, u32[]{:S(2)}) async-start(f32[64,1,640]{2,1,0:T(1,128)} %shard_map.103), calls=%async_computation | async-start | bytes 327680 | tf_op jit(solution)/shard_map/all_to_all | solution.py:854
  16.7 0.0 copy-done.1
  16.7 0.0 copy-start.2
  16.8 3.5 %collective-permute-start.2 = (f32[3,10,512]{2,1,0:T(8,128)S(1)}, f32[3,10,512]{2,1,0:T(8,128)S(1)}, u32[]{:S(2)}, u32[]{:S(2)}) collective-permute-start(f32[3,10,512]{2,1,0:T(8,128)S(1)} %get-tuple-element.39), channel_id=1, source_target_pairs={{4,8},{8,4},{12,16},{16,12},{20,24},{24,20},{28,32},{32,28},{36,40... | collective-permute-start | bytes 184328 | tf_op jit(solution)/shard_map/ppermute | solution.py:837
  20.3 0.1 collective-permute-start.1
  20.4 0.0 copy-done.2
  20.4 0.5 shard_map.104.order_ref.inv_ref
  20.9 7.5 %all-to-all-done = f32[64,1,640]{2,1,0:T(1,128)S(1)} async-done(((f32[64,1,640]{2,1,0:T(1,128)}), f32[64,1,640]{2,1,0:T(1,128)S(1)}, u32[]{:S(2)}, u32[]{:S(2)}) %all-to-all-start) | async-done | bytes 163872 | tf_op jit(solution)/shard_map/all_to_all | solution.py:854
  28.4 3.5 %shard_map.105 = (f32[3,16,512]{2,1,0:T(8,128)S(1)}, f32[3,10,512]{2,1,0:T(8,128)S(1)}, f32[3,10,512]{2,1,0:T(8,128)S(1)}, f32[152,128]{1,0:T(8,128)S(1)}, f32[3...) custom-call(f32[64,640]{1,0:T(8,128)S(1)} %bitcast.16, ...), custom_call_target="tpu_custom_call" | custom-call | tf_op jit(solution)/shard_map/pallas_call | solution.py:865
  31.9 0.5 collective-permute-start
  32.4 0.0 collective-permute-done.2.next_chip
  32.4 0.0 collective-permute-done.1.chip
  32.4 1.1 %shard_map.106 = (f32[3,4,48,128]{3,2,1,0:T(8,128)S(1)}, f32[3,4,32,128]{3,2,1,0:T(8,128)S(1)}, f32[3,4,32,128]{3,2,1,0:T(8,128)S(1)}) custom-call(f32[1,3,16,512]{3,2,1,0:T(8,128)S(1)} %copy-done.1, f32[3,10,512]{2,1,0:T(8,128)S(1)} %collective-permute-done.1.chip, f32[3,10,512]{2,1,0:T(8,128)S(1)} %collective-permute-done.2.next_chip), custom_call_target="tpu_custom_call" | custom-call | tf_op jit(solution)/shard_map/pallas_call | solution.py:856
  33.6 0.0 collective-permute-done.chip
  33.6 0.0 copy-start
  33.6 4.5 %shard_map.107 = (f32[64,1,384]{2,1,0:T(1,128)S(1)}, f32[3,16,512]{2,1,0:T(8,128)}) custom-call(f32[3,16,512]{2,1,0:T(8,128)S(1)} %get-tuple-element.21.strip_ref, f32[3,10,512]{2,1,0:T(8,128)S(1)} %collective-permute-done.chip, f32[3,10,512]{2,1,0:T(8,128)S(1)} %get-tuple-element.23.next_chip, f32[3,4,48,128]{3,2,1,0:T(8,128)S(1)} %get-tuple-element.24.ext_ref, ...), custom_call_target="tpu_custom_call" | custom-call | tf_op jit(solution)/shard_map/pallas_call | solution.py:889
  38.1 14.3 %all_to_all.10 = f32[64,1,384]{2,1,0:T(1,128)S(1)} all-to-all(f32[64,1,384]{2,1,0:T(1,128)S(1)} %get-tuple-element.35), channel_id=1, replica_groups=mesh['space'=64,'view'=4] {'space'}, dimensions={0} | all-to-all | bytes 196608 | tf_op jit(solution)/shard_map/all_to_all | solution.py:921
  52.3 1.0 %shard_map.108 = (f32[152,128]{1,0:T(8,128)S(1)}, f32[1,128]{1,0:T(1,128)}) custom-call(f32[64,384]{1,0:T(8,128)S(1)} %bitcast.17, s32[32,128]{1,0:T(8,128)S(1)} %shard_map.104.order_ref.inv_ref), custom_call_target="tpu_custom_call" | custom-call | tf_op jit(solution)/shard_map/pallas_call | solution.py:922
  53.3 2.5 %collective-permute-start.5 = (f32[152,128]{1,0:T(8,128)S(1)}, f32[152,128]{1,0:T(8,128)S(1)}, u32[]{:S(2)}, u32[]{:S(2)}) collective-permute-start(f32[152,128]{1,0:T(8,128)S(1)} %get-tuple-element.36.rec0), channel_id=1, source_target_pairs={{0,3},{1,0},{2,1},{3,2},{4,7},{5,4},{6,5},{7,6},{8,11},{9,8},{10,9... | collective-permute-start | bytes 233480 | tf_op jit(solution)/shard_map/ppermute | solution.py:928
  55.8 0.5 collective-permute-start.4
  56.3 0.6 collective-permute-start.3
  56.9 0.3 collective-permute-done.5.rec3
  57.2 3.4 %collective-permute-done.4.rec2 = f32[152,128]{1,0:T(8,128)S(1)} collective-permute-done((f32[152,128]{1,0:T(8,128)S(1)}, f32[152,128]{1,0:T(8,128)S(1)}, u32[]{:S(2)}, u32[]{:S(2)}) %collective-permute-start.4) | collective-permute-done | bytes 77856 | tf_op jit(solution)/shard_map/ppermute | solution.py:928
  60.6 2.1 %collective-permute-done.3.rec1 = f32[152,128]{1,0:T(8,128)S(1)} collective-permute-done((f32[152,128]{1,0:T(8,128)S(1)}, f32[152,128]{1,0:T(8,128)S(1)}, u32[]{:S(2)}, u32[]{:S(2)}) %collective-permute-start.3) | collective-permute-done | bytes 77856 | tf_op jit(solution)/shard_map/ppermute | solution.py:928
  62.7 0.0 copy-done
  62.7 1.4 %shard_map.109 = f32[59,2048]{1,0:T(8,128)} custom-call(f32[59,2048]{1,0:T(8,128)S(1)} %copy-done, f32[152,128]{1,0:T(8,128)S(1)} %get-tuple-element.36.rec0, f32[152,128]{1,0:T(8,128)S(1)} %collective-permute-done.3.rec1, f32[152,128]{1,0:T(8,128)S(1)} %collective-permute-done.4.rec2, f32[152,128]{1,0:T(8,128)S(1)} %collective-permute-done.5.rec3), custom_call_target="tpu_custom_call" | custom-call | tf_op jit(solution)/shard_map/pallas_call | solution.py:931
  (3 shorter events, 0.0 us)
Async XLA Ops:
  3.4 13.3 %copy-start.1 = (f32[1,3,16,512]{3,2,1,0:T(8,128)S(1)}, f32[1,3,16,512]{3,2,1,0:T(8,128)}, u32[]{:S(2)}) copy-start(f32[1,3,16,512]{3,2,1,0:T(8,128)} %own.1) | copy-start | bytes 294916
  3.4 25.0 %all-to-all-start = ((f32[64,1,640]{2,1,0:T(1,128)}), f32[64,1,640]{2,1,0:T(1,128)S(1)}, u32[]{:S(2)}, u32[]{:S(2)}) async-start(f32[64,1,640]{2,1,0:T(1,128)} %shard_map.103), calls=%async_computation | async-start | bytes 327680 | tf_op jit(solution)/shard_map/all_to_all | solution.py:854
  16.7 3.7 %copy-start.2 = (s32[1,128,16]{1,2,0:T(8,128)S(1)}, s32[1,128,16]{1,2,0:T(8,128)}, u32[]{:S(2)}) copy-start(s32[1,128,16]{1,2,0:T(8,128)} %param.9) | copy-start | bytes 24580
  16.8 15.7 %collective-permute-start.2 = (f32[3,10,512]{2,1,0:T(8,128)S(1)}, f32[3,10,512]{2,1,0:T(8,128)S(1)}, u32[]{:S(2)}, u32[]{:S(2)}) collective-permute-start(f32[3,10,512]{2,1,0:T(8,128)S(1)} %get-tuple-element.39), channel_id=1, source_target_pairs={{4,8},{8,4},{12,16},{16,12},{20,24},{24,20},{28,32},{32,28},{36,40... | collective-permute-start | bytes 184328 | tf_op jit(solution)/shard_map/ppermute | solution.py:837
  20.3 12.1 %collective-permute-start.1 = (f32[3,10,512]{2,1,0:T(8,128)S(1)}, f32[3,10,512]{2,1,0:T(8,128)S(1)}, u32[]{:S(2)}, u32[]{:S(2)}) collective-permute-start(f32[3,10,512]{2,1,0:T(8,128)S(1)} %get-tuple-element.40), channel_id=1, source_target_pairs={{0,4},{4,0},{8,12},{12,8},{16,20},{20,16},{24,28},{28,24},{32,36},... | collective-permute-start | bytes 184328 | tf_op jit(solution)/shard_map/ppermute | solution.py:836
  31.9 1.6 %collective-permute-start = (f32[3,10,512]{2,1,0:T(8,128)S(1)}, f32[3,10,512]{2,1,0:T(8,128)S(1)}, u32[]{:S(2)}, u32[]{:S(2)}) collective-permute-start(f32[3,10,512]{2,1,0:T(8,128)S(1)} %get-tuple-element.22), channel_id=1, source_target_pairs={{0,4},{4,0},{8,12},{12,8},{16,20},{20,16},{24,28},{28,24},{32,36},... | collective-permute-start | bytes 184328 | tf_op jit(solution)/shard_map/ppermute | solution.py:888
  33.6 29.2 %copy-start = (f32[59,2048]{1,0:T(8,128)S(1)}, f32[59,2048]{1,0:T(8,128)}, u32[]{:S(2)}) copy-start(f32[59,2048]{1,0:T(8,128)} %p_ref.1) | copy-start | bytes 1449988
  53.3 3.9 %collective-permute-start.5 = (f32[152,128]{1,0:T(8,128)S(1)}, f32[152,128]{1,0:T(8,128)S(1)}, u32[]{:S(2)}, u32[]{:S(2)}) collective-permute-start(f32[152,128]{1,0:T(8,128)S(1)} %get-tuple-element.36.rec0), channel_id=1, source_target_pairs={{0,3},{1,0},{2,1},{3,2},{4,7},{5,4},{6,5},{7,6},{8,11},{9,8},{10,9... | collective-permute-start | bytes 233480 | tf_op jit(solution)/shard_map/ppermute | solution.py:928
  55.8 4.8 %collective-permute-start.4 = (f32[152,128]{1,0:T(8,128)S(1)}, f32[152,128]{1,0:T(8,128)S(1)}, u32[]{:S(2)}, u32[]{:S(2)}) collective-permute-start(f32[152,128]{1,0:T(8,128)S(1)} %get-tuple-element.36.rec0), channel_id=1, source_target_pairs={{0,2},{1,3},{2,0},{3,1},{4,6},{5,7},{6,4},{7,5},{8,10},{9,11},{10,... | collective-permute-start | bytes 233480 | tf_op jit(solution)/shard_map/ppermute | solution.py:928
  56.3 6.4 %collective-permute-start.3 = (f32[152,128]{1,0:T(8,128)S(1)}, f32[152,128]{1,0:T(8,128)S(1)}, u32[]{:S(2)}, u32[]{:S(2)}) collective-permute-start(f32[152,128]{1,0:T(8,128)S(1)} %get-tuple-element.36.rec0), channel_id=1, source_target_pairs={{0,1},{1,2},{2,3},{3,0},{4,5},{5,6},{6,7},{7,4},{8,9},{9,10},{10,1... | collective-permute-start | bytes 233480 | tf_op jit(solution)/shard_map/ppermute | solution.py:928

commit v4 on v3

--- a/solution.py
+++ b/solution.py
@@ -60,8 +60,11 @@
 
 
 def turn_of(angles):
-    cos_a, cos_b, cos_c = (jnp.cos(angle) for angle in angles)
-    sin_a, sin_b, sin_c = (jnp.sin(angle) for angle in angles)
+    count = angles[0].shape[0]
+    stacked = jnp.concatenate(angles, axis=0)
+    cosines, sines = jnp.cos(stacked), jnp.sin(stacked)
+    cos_a, cos_b, cos_c = (cosines[i * count : (i + 1) * count] for i in range(3))
+    sin_a, sin_b, sin_c = (sines[i * count : (i + 1) * count] for i in range(3))
     return [
         [cos_c * cos_b, cos_c * sin_b * sin_a - sin_c * cos_a, cos_c * sin_b * cos_a + sin_c * sin_a],
         [sin_c * cos_b, sin_c * sin_b * sin_a + cos_c * cos_a, sin_c * sin_b * cos_a - cos_c * sin_a],
@@ -92,12 +95,14 @@
     ]
 
 
-def camera_values(rows):
-    angles = [jnp.broadcast_to(row, (8, LANES)) for row in rows]
+def camera_values(angles):
     turn = turn_of(angles)
     basis = harmonics(turn[2])
-    cell = lambda value: value[0:1, 0:1]
-    return [[cell(value) for value in line] for line in turn], [cell(value) for value in basis]
+    cell = lambda value, v: value[v : v + 1, :]
+    return [
+        ([[cell(value, v) for value in line] for line in turn], [cell(value, v) for value in basis])
+        for v in range(angles[0].shape[0])
+    ]
 
 
 def load_params(p_ref, scratch, tiles=8):
@@ -203,7 +208,7 @@
     load_params(p_ref, par)
     spread = lambda ref: [jnp.broadcast_to(ref[0:1, i : i + 1], (1, LANES)) for i in range(3)]
     angles = spread(cam_ref)
-    turn, basis = camera_values(angles)
+    ((turn, basis),) = camera_values(angles)
     get = lambda index: dense_row(par, index)
     scales = [jnp.exp(get(3 + i)) for i in range(3)]
     quaternion, _ = unit([get(6 + i) for i in range(4)])
@@ -733,10 +738,12 @@
     quaternion, inverse_norm = unit([get(6 + i) for i in range(4)])
     spin = spin_of(quaternion)
     coefficients = []
-    angles = [
-        [views[v, META + 5 + i : META + 6 + i, :] for i in range(3)] for v in range(4)
-    ]
-    cameras = [camera_values(angles[v]) for v in range(4)]
+    cameras = camera_values(
+        [
+            jnp.concatenate([views[v, META + 5 + i : META + 6 + i, :] for v in range(4)], axis=0)
+            for i in range(3)
+        ]
+    )
     for k in range(16):
         for c in range(3):
             rows = slice(96 + 16 * c, 112 + 16 * c)

time: 64.4 us -> 64.1 us (level)
  no operation moved by 1% of the time
where the time goes in v4:
time: 64.1 us; the launch traced here: 63.8 us
  starting transfers between devices  21 us (33%)
  Pallas kernels  14.4 us (22%)
  blocking collectives  14.3 us (22%)
  waiting for transfers between devices  13.3 us (21%)
  between operations  0.77 us (1%)
    all_to_all x1, blocking collectives, shards(): returned = lax.all_to_all(reply, 'space', 0, 0, tiled=True).reshape(64, 384)  14.3 us
    all_to_all x1, starting transfers between devices, shards(): lax.all_to_all(message, 'space', 0, 0, tiled=True).reshape(64, 640)  13.3 us
    all_to_all x1, waiting for transfers between devices, shards(): lax.all_to_all(message, 'space', 0, 0, tiled=True).reshape(64, 640)  7.52 us
    ppermute x3, waiting for transfers between devices, shards(): lax.ppermute(record_grads, 'view', [(i, (i + d) % views) for i in range(v...  5.81 us
    pallas_call x1, Pallas kernels, shards(): call(loss_kernel, [((64, 1, 384), F32), ((3, 16, 512), F32)], [((CHUNKS,...  4.46 us
    ppermute x3, starting transfers between devices, shards(): lax.ppermute(record_grads, 'view', [(i, (i + d) % views) for i in range(v...  3.6 us
    ppermute x1, starting transfers between devices, shards(): lax.ppermute(jnp.where(even, goal_top, goal_bottom), 'space', next_chip)  3.54 us
    pallas_call x1, Pallas kernels, shards(): call(blend_kernel, [((3, 16, 512), F32), ((3, 10, 512), F32), ((3, 10, 51...  3.51 us
  transfers between devices with their start and end apart: 7, of which 4 were waited for; matrix products, arithmetic and copies ran while one was open for 0% of the time, Pallas kernels for 8%

profile of v4, /device:TPU:1, one launch (start us, length us, event | category | flops | bytes accessed | tf_op | source)
XLA Modules:
  0.0 63.8 jit_solution(14340952621059722673)
XLA Ops:
  0.6 2.7 %shard_map.103 = f32[64,1,640]{2,1,0:T(1,128)} custom-call(f32[59,2048]{1,0:T(8,128)} %p_ref.1, f32[1,3]{1,0:T(1,128)} %cam_hbm.1, s32[16,128]{1,0:T(8,128)} %bitcast.18, s32[1,128]{1,0:T(1,128)} %blk_hbm.1, s32[1,64]{1,0:T(1,128)} %cnt_hbm.1, s32[1,64]{1,0:T(1,128)} %rank_hbm.1, f32[1,3]{1,0:T(1,128)} %bg_hbm.1), custom_call_target="tpu_custom_call" | custom-call | tf_op jit(solution)/shard_map/pallas_call | solution.py:845
  3.3 0.0 copy-start.1
  3.4 13.3 %all-to-all-start = ((f32[64,1,640]{2,1,0:T(1,128)}), f32[64,1,640]{2,1,0:T(1,128)S(1)}, u32[]{:S(2)}, u32[]{:S(2)}) async-start(f32[64,1,640]{2,1,0:T(1,128)} %shard_map.103), calls=%async_computation | async-start | bytes 327680 | tf_op jit(solution)/shard_map/all_to_all | solution.py:861
  16.7 0.0 copy-done.1
  16.7 0.0 copy-start.2
  16.7 3.5 %collective-permute-start.2 = (f32[3,10,512]{2,1,0:T(8,128)S(1)}, f32[3,10,512]{2,1,0:T(8,128)S(1)}, u32[]{:S(2)}, u32[]{:S(2)}) collective-permute-start(f32[3,10,512]{2,1,0:T(8,128)S(1)} %get-tuple-element.39), channel_id=1, source_target_pairs={{4,8},{8,4},{12,16},{16,12},{20,24},{24,20},{28,32},{32,28},{36,40... | collective-permute-start | bytes 184328 | tf_op jit(solution)/shard_map/ppermute | solution.py:844
  20.3 0.1 collective-permute-start.1
  20.4 0.0 copy-done.2
  20.4 0.5 shard_map.104.order_ref.inv_ref
  20.8 7.5 %all-to-all-done = f32[64,1,640]{2,1,0:T(1,128)S(1)} async-done(((f32[64,1,640]{2,1,0:T(1,128)}), f32[64,1,640]{2,1,0:T(1,128)S(1)}, u32[]{:S(2)}, u32[]{:S(2)}) %all-to-all-start) | async-done | bytes 163872 | tf_op jit(solution)/shard_map/all_to_all | solution.py:861
  28.4 3.5 %shard_map.105 = (f32[3,16,512]{2,1,0:T(8,128)S(1)}, f32[3,10,512]{2,1,0:T(8,128)S(1)}, f32[3,10,512]{2,1,0:T(8,128)S(1)}, f32[152,128]{1,0:T(8,128)S(1)}, f32[3...) custom-call(f32[64,640]{1,0:T(8,128)S(1)} %bitcast.16, ...), custom_call_target="tpu_custom_call" | custom-call | tf_op jit(solution)/shard_map/pallas_call | solution.py:872
  31.9 0.5 collective-permute-start
  32.4 0.0 collective-permute-done.2.next_chip
  32.4 0.0 collective-permute-done.1.chip
  32.4 1.1 %shard_map.106 = (f32[3,4,48,128]{3,2,1,0:T(8,128)S(1)}, f32[3,4,32,128]{3,2,1,0:T(8,128)S(1)}, f32[3,4,32,128]{3,2,1,0:T(8,128)S(1)}) custom-call(f32[1,3,16,512]{3,2,1,0:T(8,128)S(1)} %copy-done.1, f32[3,10,512]{2,1,0:T(8,128)S(1)} %collective-permute-done.1.chip, f32[3,10,512]{2,1,0:T(8,128)S(1)} %collective-permute-done.2.next_chip), custom_call_target="tpu_custom_call" | custom-call | tf_op jit(solution)/shard_map/pallas_call | solution.py:863
  33.5 0.0 collective-permute-done.chip
  33.5 0.0 copy-start
  33.5 4.5 %shard_map.107 = (f32[64,1,384]{2,1,0:T(1,128)S(1)}, f32[3,16,512]{2,1,0:T(8,128)}) custom-call(f32[3,16,512]{2,1,0:T(8,128)S(1)} %get-tuple-element.21.strip_ref, f32[3,10,512]{2,1,0:T(8,128)S(1)} %collective-permute-done.chip, f32[3,10,512]{2,1,0:T(8,128)S(1)} %get-tuple-element.23.next_chip, f32[3,4,48,128]{3,2,1,0:T(8,128)S(1)} %get-tuple-element.24.ext_ref, ...), custom_call_target="tpu_custom_call" | custom-call | tf_op jit(solution)/shard_map/pallas_call | solution.py:896
  38.0 14.3 %all_to_all.10 = f32[64,1,384]{2,1,0:T(1,128)S(1)} all-to-all(f32[64,1,384]{2,1,0:T(1,128)S(1)} %get-tuple-element.35), channel_id=1, replica_groups=mesh['space'=64,'view'=4] {'space'}, dimensions={0} | all-to-all | bytes 196608 | tf_op jit(solution)/shard_map/all_to_all | solution.py:928
  52.3 1.0 %shard_map.108 = (f32[152,128]{1,0:T(8,128)S(1)}, f32[1,128]{1,0:T(1,128)}) custom-call(f32[64,384]{1,0:T(8,128)S(1)} %bitcast.17, s32[32,128]{1,0:T(8,128)S(1)} %shard_map.104.order_ref.inv_ref), custom_call_target="tpu_custom_call" | custom-call | tf_op jit(solution)/shard_map/pallas_call | solution.py:929
  53.3 2.5 %collective-permute-start.5 = (f32[152,128]{1,0:T(8,128)S(1)}, f32[152,128]{1,0:T(8,128)S(1)}, u32[]{:S(2)}, u32[]{:S(2)}) collective-permute-start(f32[152,128]{1,0:T(8,128)S(1)} %get-tuple-element.36.rec0), channel_id=1, source_target_pairs={{0,3},{1,0},{2,1},{3,2},{4,7},{5,4},{6,5},{7,6},{8,11},{9,8},{10,9... | collective-permute-start | bytes 233480 | tf_op jit(solution)/shard_map/ppermute | solution.py:935
  55.8 0.5 collective-permute-start.4
  56.3 0.6 collective-permute-start.3
  56.9 0.3 collective-permute-done.5.rec3
  57.2 3.4 %collective-permute-done.4.rec2 = f32[152,128]{1,0:T(8,128)S(1)} collective-permute-done((f32[152,128]{1,0:T(8,128)S(1)}, f32[152,128]{1,0:T(8,128)S(1)}, u32[]{:S(2)}, u32[]{:S(2)}) %collective-permute-start.4) | collective-permute-done | bytes 77856 | tf_op jit(solution)/shard_map/ppermute | solution.py:935
  60.6 2.1 %collective-permute-done.3.rec1 = f32[152,128]{1,0:T(8,128)S(1)} collective-permute-done((f32[152,128]{1,0:T(8,128)S(1)}, f32[152,128]{1,0:T(8,128)S(1)}, u32[]{:S(2)}, u32[]{:S(2)}) %collective-permute-start.3) | collective-permute-done | bytes 77856 | tf_op jit(solution)/shard_map/ppermute | solution.py:935
  62.7 0.0 copy-done
  62.7 1.1 %shard_map.109 = f32[59,2048]{1,0:T(8,128)} custom-call(f32[59,2048]{1,0:T(8,128)S(1)} %copy-done, f32[152,128]{1,0:T(8,128)S(1)} %get-tuple-element.36.rec0, f32[152,128]{1,0:T(8,128)S(1)} %collective-permute-done.3.rec1, f32[152,128]{1,0:T(8,128)S(1)} %collective-permute-done.4.rec2, f32[152,128]{1,0:T(8,128)S(1)} %collective-permute-done.5.rec3), custom_call_target="tpu_custom_call" | custom-call | tf_op jit(solution)/shard_map/pallas_call | solution.py:938
  (3 shorter events, 0.0 us)
Async XLA Ops:
  3.3 13.3 %copy-start.1 = (f32[1,3,16,512]{3,2,1,0:T(8,128)S(1)}, f32[1,3,16,512]{3,2,1,0:T(8,128)}, u32[]{:S(2)}) copy-start(f32[1,3,16,512]{3,2,1,0:T(8,128)} %own.1) | copy-start | bytes 294916
  3.4 25.0 %all-to-all-start = ((f32[64,1,640]{2,1,0:T(1,128)}), f32[64,1,640]{2,1,0:T(1,128)S(1)}, u32[]{:S(2)}, u32[]{:S(2)}) async-start(f32[64,1,640]{2,1,0:T(1,128)} %shard_map.103), calls=%async_computation | async-start | bytes 327680 | tf_op jit(solution)/shard_map/all_to_all | solution.py:861
  16.7 3.7 %copy-start.2 = (s32[1,128,16]{1,2,0:T(8,128)S(1)}, s32[1,128,16]{1,2,0:T(8,128)}, u32[]{:S(2)}) copy-start(s32[1,128,16]{1,2,0:T(8,128)} %param.9) | copy-start | bytes 24580
  16.7 15.7 %collective-permute-start.2 = (f32[3,10,512]{2,1,0:T(8,128)S(1)}, f32[3,10,512]{2,1,0:T(8,128)S(1)}, u32[]{:S(2)}, u32[]{:S(2)}) collective-permute-start(f32[3,10,512]{2,1,0:T(8,128)S(1)} %get-tuple-element.39), channel_id=1, source_target_pairs={{4,8},{8,4},{12,16},{16,12},{20,24},{24,20},{28,32},{32,28},{36,40... | collective-permute-start | bytes 184328 | tf_op jit(solution)/shard_map/ppermute | solution.py:844
  20.3 12.1 %collective-permute-start.1 = (f32[3,10,512]{2,1,0:T(8,128)S(1)}, f32[3,10,512]{2,1,0:T(8,128)S(1)}, u32[]{:S(2)}, u32[]{:S(2)}) collective-permute-start(f32[3,10,512]{2,1,0:T(8,128)S(1)} %get-tuple-element.40), channel_id=1, source_target_pairs={{0,4},{4,0},{8,12},{12,8},{16,20},{20,16},{24,28},{28,24},{32,36},... | collective-permute-start | bytes 184328 | tf_op jit(solution)/shard_map/ppermute | solution.py:843
  31.9 1.6 %collective-permute-start = (f32[3,10,512]{2,1,0:T(8,128)S(1)}, f32[3,10,512]{2,1,0:T(8,128)S(1)}, u32[]{:S(2)}, u32[]{:S(2)}) collective-permute-start(f32[3,10,512]{2,1,0:T(8,128)S(1)} %get-tuple-element.22), channel_id=1, source_target_pairs={{0,4},{4,0},{8,12},{12,8},{16,20},{20,16},{24,28},{28,24},{32,36},... | collective-permute-start | bytes 184328 | tf_op jit(solution)/shard_map/ppermute | solution.py:895
  33.5 29.2 %copy-start = (f32[59,2048]{1,0:T(8,128)S(1)}, f32[59,2048]{1,0:T(8,128)}, u32[]{:S(2)}) copy-start(f32[59,2048]{1,0:T(8,128)} %p_ref.1) | copy-start | bytes 1449988
  53.3 3.9 %collective-permute-start.5 = (f32[152,128]{1,0:T(8,128)S(1)}, f32[152,128]{1,0:T(8,128)S(1)}, u32[]{:S(2)}, u32[]{:S(2)}) collective-permute-start(f32[152,128]{1,0:T(8,128)S(1)} %get-tuple-element.36.rec0), channel_id=1, source_target_pairs={{0,3},{1,0},{2,1},{3,2},{4,7},{5,4},{6,5},{7,6},{8,11},{9,8},{10,9... | collective-permute-start | bytes 233480 | tf_op jit(solution)/shard_map/ppermute | solution.py:935
  55.8 4.8 %collective-permute-start.4 = (f32[152,128]{1,0:T(8,128)S(1)}, f32[152,128]{1,0:T(8,128)S(1)}, u32[]{:S(2)}, u32[]{:S(2)}) collective-permute-start(f32[152,128]{1,0:T(8,128)S(1)} %get-tuple-element.36.rec0), channel_id=1, source_target_pairs={{0,2},{1,3},{2,0},{3,1},{4,6},{5,7},{6,4},{7,5},{8,10},{9,11},{10,... | collective-permute-start | bytes 233480 | tf_op jit(solution)/shard_map/ppermute | solution.py:935
  56.3 6.4 %collective-permute-start.3 = (f32[152,128]{1,0:T(8,128)S(1)}, f32[152,128]{1,0:T(8,128)S(1)}, u32[]{:S(2)}, u32[]{:S(2)}) collective-permute-start(f32[152,128]{1,0:T(8,128)S(1)} %get-tuple-element.36.rec0), channel_id=1, source_target_pairs={{0,1},{1,2},{2,3},{3,0},{4,5},{5,6},{6,7},{7,4},{8,9},{9,10},{10,1... | collective-permute-start | bytes 233480 | tf_op jit(solution)/shard_map/ppermute | solution.py:935
